TPU v7x, 256 devices: a whole 4x4x8 slice. The times are simulated.
256 devices in a mesh: net: 16 (over z, x_hi), mem: 16 (over x_lo, y, core).
Axes of the slice: x: 4 (x_hi: 2, x_lo: 2; x = x_hi * 2 + x_lo), y: 4, z: 8, core: 2. Of those that a mesh axis runs over, the one named last changes fastest.
Arguments:
- stored_reach_flows: bfloat16 [5, 512, 65536], P(None, 'mem', 'net'), may hold values from 0.19921875 to 5
- lateral: bfloat16 [4, 512, 65536], P(None, 'mem', 'net'), may hold values from 0.049804688 to 1
- cotangent: bfloat16 [4, 512, 65536], P(None, 'mem', 'net'), may hold values from -3 to 3
- roughness: float32 [65536], P('net'), may hold values from 0.02 to 0.1
- travel_factor: float32 [65536], P('net'), may hold values from 0.2 to 5
- inverse_block_matrix: float32 [512, 128, 128], P('net'), may hold values from 0 to 1, as said below
- down_in_block: int32 [65536], P('net'), may hold values from 1 to 128, as said below
- exit_slot: int32 [65536], P('net'), may hold values from -1 to 127, as said below
- inlet_reach: int32 [16, 128], P('net'), may hold values from 1 to 3999, as said below
Outputs:
- grad_lateral: bfloat16 [4, 512, 65536], P(None, 'mem', 'net')
- grad_rough: float32 [65536], P(('net', 'mem'))
Inputs may be any that keep to these rules, and one draw needn't show every extreme that they name: Within a block a reach feeds a later position: down_in_block[r] > r % 128 where it is under 128. exit_slot[r] >= 0 only where down_in_block[r] == 128 and r is not in the last partition; every reach of the last partition has -1. `inlet_reach`: each entry is a reach at positions 1 to 31 of some block of that partition; several slots may name the same reach. inverse_block_matrix[k][i, j] is 1 where i = j, the product of weight_new over the reaches after j up to and including i where i lies on the in-block path of next reaches from j, and 0 elsewhere.
All inputs are finite; a program needn't handle non-finite values.
Results may differ from a plain program's by a relative error of at most 0.001.
Values sent between devices are 32-bit elements; how exact they have to be, the bound alone decides.
A program may use at most 64 MiB of HBM per device.

v0:
```python
import jax
import jax.numpy as jnp
from jax import lax
from jax.sharding import PartitionSpec as P

skew_weight = 0.2


def from_behind(value, axis, by):
    count = lax.axis_size(axis)
    pairs = [(i, i + by) for i in range(count) if 0 <= i + by < count]
    return lax.ppermute(value, axis, pairs)


def coefficients(roughness, travel_factor):
    travel = roughness * travel_factor
    divisor = travel * (1.0 - skew_weight) + 0.5
    weight_new = (0.5 - travel * skew_weight) / divisor
    weight_old = (0.5 + travel * skew_weight) / divisor
    weight_stay = (travel * (1.0 - skew_weight) - 0.5) / divisor
    weight_side = 1.0 / divisor
    square = divisor * divisor
    updated_slope = -0.5 / square
    slope_old = (skew_weight - 0.5) / square
    slope_stay = (1.0 - skew_weight) / square
    slope_side = (skew_weight - 1.0) / square
    return (
        (weight_new, weight_old, weight_stay, weight_side),
        (updated_slope, slope_old, slope_stay, slope_side),
    )


def solve_blocks(right_side, inverse_block_matrix):
    members, reaches = right_side.shape
    reshaped_values = right_side.reshape(members, reaches // 128, 128)
    solved_adjoint = jnp.einsum(
        "acj,cjv->acv", reshaped_values, inverse_block_matrix, precision=lax.Precision.HIGHEST
    )
    return solved_adjoint.reshape(members, reaches)


def body(
    stored_reach_flows,
    lateral,
    cotangent,
    roughness,
    travel_factor,
    inverse_block_matrix,
    down_in_block,
    exit_slot,
    inlet_reach,
):
    step_count = cotangent.shape[0]
    members = stored_reach_flows.shape[1]
    reaches = stored_reach_flows.shape[2]
    blocks = reaches // 128
    slot_count = inlet_reach.shape[1]
    weights, slopes = coefficients(roughness, travel_factor)
    weight_new, weight_old, weight_stay, weight_side = weights
    updated_slope, slope_old, slope_stay, slope_side = slopes
    positions = jnp.arange(128, dtype=jnp.int32)
    within_table = down_in_block.reshape(blocks, 128)[:, :, None] == positions[None, None, :]
    within = within_table.astype(jnp.bfloat16)
    exact_within_partition = within_table.astype(jnp.float32)
    local_in = jnp.einsum(
        "lmbu,bur->lmbr",
        stored_reach_flows.reshape(step_count + 1, members, blocks, 128),
        within,
        preferred_element_type=jnp.float32,
    ).reshape(step_count + 1, members, reaches)
    slot_table = exit_slot[:, None] == jnp.arange(slot_count, dtype=jnp.int32)[None, :]
    leaving_flow = slot_table.astype(jnp.bfloat16)
    leaving_exact = slot_table.astype(jnp.float32).T
    reach_outflow = jnp.einsum(
        "gcq,qj->gcj", stored_reach_flows, leaving_flow, preferred_element_type=jnp.float32
    )
    arriving_flow = from_behind(reach_outflow, "net", 1)
    inlets = inlet_reach[0]
    placement_rows = (inlets[:, None] == jnp.arange(reaches, dtype=jnp.int32)[None, :]).astype(
        jnp.float32
    )
    inflow = local_in + jnp.einsum(
        "dqe,ej->dqj", arriving_flow, placement_rows, precision=lax.Precision.HIGHEST
    )
    weight_new_in = weight_new[inlets]
    weight_old_in = weight_old[inlets]

    def from_below(values):
        return jnp.dot(
            values,
            leaving_exact,
            precision=lax.Precision.HIGHEST,
            preferred_element_type=jnp.float32,
        )

    def inlet_rows(adjoint):
        adjoint_inlet = jnp.einsum(
            "mr,er->me", adjoint, placement_rows, precision=lax.Precision.HIGHEST
        )
        return jnp.stack([weight_new_in * adjoint_inlet, weight_old_in * adjoint_inlet])

    zero_slots = jnp.zeros((members, slot_count), jnp.float32)
    running = jnp.zeros((reaches,), jnp.float32)
    adjoint_next = jnp.zeros((members, reaches), jnp.float32)
    remote_prior = zero_slots
    outputs = [None] * step_count
    for counter in range(step_count):
        current_instant = step_count - counter
        weighted_flows = (weight_old * adjoint_next).reshape(members, blocks, 128)
        interior_reaches = jnp.einsum(
            "qvt,vzt->qvz", weighted_flows, exact_within_partition, precision=lax.Precision.HIGHEST
        )
        source = (
            cotangent[current_instant - 1].astype(jnp.float32)
            + weight_stay * adjoint_next
            + (interior_reaches.reshape(members, reaches) + from_below(remote_prior))
        )

        def one_section(section_id, carry):
            adjoint, remote_new, remote_old = carry
            adjoint = solve_blocks(source + from_below(remote_new), inverse_block_matrix)
            received = from_behind(inlet_rows(adjoint), "net", -1)
            return (adjoint, received[0], received[1])

        adjoint, remote_new, remote_old = lax.fori_loop(
            0,
            lax.axis_size("net"),
            one_section,
            (jnp.zeros_like(adjoint_next), zero_slots, zero_slots),
        )
        inflow_now = lax.dynamic_index_in_dim(inflow, current_instant, 0, False)
        inflow_prior = lax.dynamic_index_in_dim(inflow, current_instant - 1, 0, False)
        flows_prior = lax.dynamic_index_in_dim(
            stored_reach_flows, current_instant - 1, 0, False
        ).astype(jnp.float32)
        forcing = lax.dynamic_index_in_dim(lateral, current_instant - 1, 0, False).astype(
            jnp.float32
        )
        factor = (
            updated_slope * inflow_now
            + slope_old * inflow_prior
            + slope_stay * flows_prior
            + slope_side * forcing
        )
        part_sum = jnp.sum(adjoint * factor, axis=0)
        lateral_grad = (weight_side * adjoint).astype(jnp.bfloat16)
        running = running + part_sum
        outputs[current_instant - 1] = lateral_grad
        adjoint_next = adjoint
        remote_prior = remote_old
    grad_lateral = jnp.stack(outputs)
    grad_rough = lax.psum_scatter(travel_factor * running, "mem", scatter_dimension=0, tiled=True)
    return (grad_lateral, grad_rough)


def solution(mesh):
    in_specs = (
        P(None, "mem", "net"),
        P(None, "mem", "net"),
        P(None, "mem", "net"),
        P("net"),
        P("net"),
        P("net", None, None),
        P("net"),
        P("net"),
        P("net", None),
    )
    out_specs = (P(None, "mem", "net"), P(("net", "mem")))
    return jax.shard_map(body, mesh=mesh, in_specs=in_specs, out_specs=out_specs, check_vma=False)
```

profile of v0, /device:TPU:102, one launch (start us, length us, event | category | flops | bytes accessed | tf_op | source)
XLA Modules:
  0.0 1155.0 jit_solution(18129467379094753171)
XLA Ops:
  28.0 261.2 %while.58 = (s32[]{:T(128)}, f32[32,4096]{1,0:T(8,128)}, f32[32,128]{1,0:T(8,128)S(1)}, f32[32,128]{1,0:T(8,128)}, f32[32,4096]{1,0:T(8,128)S(1)}, /*index=5*/f3...) while((s32[]{:T(128)}, f32[32,4096]{1,0:T(8,128)}, ...), condition=%wide.region_1.0_spmd.clone, body=%wide.region_0.0_spmd.clone.sunk | while | flops 606224384 | bytes 8193713 | solution.py:125
  36.2 7.5 collective-permute-done
  52.5 7.5 collective-permute-done
  68.8 7.5 collective-permute-done
  85.1 7.5 collective-permute-done
  101.4 7.5 collective-permute-done
  117.7 7.5 collective-permute-done
  134.0 7.5 collective-permute-done
  150.3 7.5 collective-permute-done
  166.6 7.5 collective-permute-done
  182.9 7.5 collective-permute-done
  199.3 7.5 collective-permute-done
  215.6 7.5 collective-permute-done
  231.9 7.8 collective-permute-done
  248.5 7.5 collective-permute-done
  264.8 7.5 collective-permute-done
  281.1 7.5 collective-permute-done
  298.1 260.9 %while.59 = (s32[]{:T(128)}, f32[32,4096]{1,0:T(8,128)}, f32[32,128]{1,0:T(8,128)S(1)}, f32[32,128]{1,0:T(8,128)}, f32[32,4096]{1,0:T(8,128)S(1)}, /*index=5*/f3...) while((s32[]{:T(128)}, f32[32,4096]{1,0:T(8,128)}, ...), condition=%wide.region_3.4_spmd.clone, body=%wide.region_2.3_spmd.clone.sunk | while | flops 606224384 | bytes 8193713 | solution.py:125
  306.3 7.5 collective-permute-done.1
  436.8 7.5 collective-permute-done.1
  469.4 7.5 collective-permute-done.1
  566.1 261.0 %while.60 = (s32[]{:T(128)}, f32[32,4096]{1,0:T(8,128)}, f32[32,128]{1,0:T(8,128)S(1)}, f32[32,128]{1,0:T(8,128)}, f32[32,4096]{1,0:T(8,128)S(1)}, /*index=5*/f3...) while((s32[]{:T(128)}, f32[32,4096]{1,0:T(8,128)}, ...), condition=%wide.region_5.6_spmd.clone, body=%wide.region_4.5_spmd.clone.sunk | while | flops 606224384 | bytes 8193713 | solution.py:125
  590.6 7.5 collective-permute-done.2
  688.4 7.5 collective-permute-done.2
  704.7 7.5 collective-permute-done.2
  786.3 7.7 collective-permute-done.2
  833.9 263.3 %while.61 = (s32[]{:T(128)}, f32[32,4096]{1,0:T(8,128)}, f32[32,128]{1,0:T(8,128)S(1)}, f32[32,4096]{1,0:T(8,128)S(1)}, f32[32,128,128]{2,1,0:T(8,128)S(1)}, /*i...) while((s32[]{:T(128)}, f32[32,4096]{1,0:T(8,128)}, ...), condition=%wide.region_7.8_spmd.clone, body=%wide.region_6.7_spmd.clone.sunk | while | flops 606224384 | bytes 8160937 | solution.py:125
  859.3 7.5 collective-permute-done.3
  958.0 7.5 collective-permute-done.3
  974.5 7.5 collective-permute-done.3
  1073.2 7.5 collective-permute-done.3
  1100.3 52.9 %all-reduce = f32[4096]{0:T(1024)S(1)} all-reduce(f32[4096]{0:T(1024)S(1)} %add_multiply_fusion), channel_id=2, replica_groups=mesh['net'=16,'mem'=16] {'mem'}, use_global_device_ids=true, to_apply=%region_12.13.clone | all-reduce | flops 4096 | bytes 32768
  (688 shorter events, 894.4 us)
Async XLA Ops:
  3.0 18.8 %collective-permute-start.4 = (f32[5,32,128]{2,1,0:T(8,128)S(1)}, f32[5,32,128]{2,1,0:T(8,128)S(1)}, u32[]{:S(2)}, u32[]{:S(2)}) collective-permute-start(f32[5,32,128]{2,1,0:T(8,128)S(1)} %fusion.74), channel_id=1, source_target_pairs={{0,16},{16,32},{32,48},{48,64},{64,80},{80,96},{96,112},{112,128},... | collective-permute-start | bytes 245768 | tf_op jit(solution)/shard_map/ppermute | solution.py:12
  34.3 9.4 collective-permute-start
  50.6 9.4 collective-permute-start
  66.9 9.4 collective-permute-start
  83.2 9.4 collective-permute-start
  99.5 9.4 collective-permute-start
  115.8 9.4 collective-permute-start
  132.1 9.4 collective-permute-start
  148.4 9.4 collective-permute-start
  164.7 9.4 collective-permute-start
  181.0 9.4 collective-permute-start
  197.3 9.4 collective-permute-start
  213.6 9.4 collective-permute-start
  229.9 9.7 collective-permute-start
  246.6 9.4 collective-permute-start
  262.9 9.4 collective-permute-start
  279.2 9.4 collective-permute-start
  304.4 9.4 collective-permute-start.1
  320.7 9.4 collective-permute-start.1
  434.8 9.4 collective-permute-start.1
  451.1 9.4 collective-permute-start.1
  467.4 9.4 collective-permute-start.1
  588.7 9.4 collective-permute-start.2
  670.2 9.4 collective-permute-start.2
  686.5 9.4 collective-permute-start.2
  702.8 9.4 collective-permute-start.2
  784.3 9.6 collective-permute-start.2
  857.4 9.4 collective-permute-start.3
  956.1 9.4 collective-permute-start.3
  972.6 9.4 collective-permute-start.3
  1054.8 9.4 collective-permute-start.3
  1071.3 9.4 collective-permute-start.3
  (116 other events, 2923.2 us)
where the time goes:
time: 1160 us; the launch traced here: 1150 us
  waiting for transfers between devices  480 us (41%)
  matrix products  426 us (37%)
  starting transfers between devices  129 us (11%)
  local copies, waits for them, and re-layouts  54.3 us (5%)
  blocking collectives  52.9 us (5%)
    ppermute x65, waiting for transfers between devices, from_behind(): return lax.ppermute(value, axis, pairs)  480 us
    dot_general x64, matrix products, inlet_rows(): jnp.einsum('mr,er->me', adjoint, placement_rows, precision=lax.Precision....  184 us
    ppermute x65, starting transfers between devices, from_behind(): return lax.ppermute(value, axis, pairs)  129 us
    dot_general x64, matrix products, solve_blocks(): jnp.einsum('acj,cjv->acv', reshaped_values, inverse_block_matrix, precisi...  122 us
    dot_general x68, matrix products, from_below(): jnp.dot(values, leaving_exact, precision=lax.Precision.HIGHEST, preferred...  100 us
    unnamed x1, blocking collectives  52.9 us
    squeeze x64, local copies, waits for them, and re-layouts, one_section(): return (adjoint, received[0], received[1])  28.9 us
  transfers between devices with their start and end apart: 65, of which 64 were waited for; matrix products, arithmetic and copies ran while one was open for 1% of the time, Pallas kernels for 0%

commit v1 on v0

v1 whole, which is shorter than its diff:
```python
import jax
import jax.numpy as jnp
from jax import lax
from jax.experimental import pallas as pl
from jax.experimental.pallas import tpu as pltpu
from jax.sharding import PartitionSpec as P

F32, BF16 = jnp.float32, jnp.bfloat16
LANES = 128
GROUP = 8
MESH = pl.DeviceIdType.MESH


def dot(a, b):
    return lax.dot_general(a, b, (((1,), (0,)), ((), ())), preferred_element_type=F32)


def dot_t(a, b):
    return lax.dot_general(a, b, (((1,), (1,)), ((), ())), preferred_element_type=F32)


def split(value):
    high = value.astype(BF16)
    return high, (value - high.astype(F32)).astype(BF16)


def rows_of(rows, count=8):
    place = lax.broadcasted_iota(jnp.int32, (count, LANES), 0)
    out = jnp.zeros((count, LANES), F32)
    for i, row in enumerate(rows):
        out = jnp.where(place == i, jnp.broadcast_to(row, (count, LANES)), out)
    return out


def one_hot(row, start):
    place = lax.broadcasted_iota(jnp.int32, (LANES, LANES), 0) + start
    return jnp.where(place == row, 1.0, 0.0).astype(BF16)


def local_kernel(
    cot_ref, flow_ref, rough_ref, factor_ref, exit_ref, matrix_ref, inlet_ref,
    local_ref, gain_ref, inner_ref, leaving_ref,
):
    step = pl.program_id(0)
    steps, members = cot_ref.shape[0], cot_ref.shape[1]
    inlet = inlet_ref[...]
    inner = jnp.zeros((2 * (steps * members + 8), LANES), F32)
    leaving = jnp.zeros(leaving_ref.shape, F32)
    for j in range(GROUP):
        lanes = slice(j * LANES, (j + 1) * LANES)
        travel = rough_ref[j : j + 1, :] * factor_ref[j : j + 1, :]
        divisor = 0.8 * travel + 0.5
        numer_new = 0.5 - 0.2 * travel
        numer_old = 0.5 + 0.2 * travel
        weight_new = numer_new / divisor
        weight_old = numer_old / divisor
        ratio = numer_old / numer_new
        carry = (0.8 * travel - 0.5) / divisor + ratio
        exits = exit_ref[j : j + 1, :]
        matrix = matrix_ref[j]
        high, low = split(matrix)
        pattern = jnp.where(matrix != 0.0, 1.0, 0.0).astype(BF16)
        opened = jnp.where(exits >= 0, 1.0, 0.0)
        numbered = rows_of([jnp.where(exits >= 0, exits + 1, 0).astype(F32)])
        slot = dot(numbered.astype(BF16), pattern)[0:1]
        adjoint = None
        found = [None] * steps
        gains = []
        for t in reversed(range(steps)):
            start = cot_ref[t, :, lanes].astype(F32)
            if adjoint is None:
                x = jnp.concatenate([start, rows_of([opened])], 0).astype(BF16)
                adjoint = dot(x, high) + dot(x, low)
            else:
                x = jnp.concatenate([start, jnp.zeros((8, LANES), F32)], 0) + adjoint * carry
                x_high, x_low = split(x)
                adjoint = dot(x_high, high) + dot(x_low, high) + dot(x_high, low) - adjoint * ratio
            found[t] = adjoint[:members]
            local_ref[t, :, lanes] = adjoint[:members]
            gains.append(adjoint[members : members + 1])
        facts = rows_of(gains + [slot, weight_new, weight_old])
        gain_ref[:, lanes] = facts
        stacked = jnp.concatenate(found + [facts], 0)
        stacked_high = stacked.astype(BF16).astype(F32)
        both = jnp.concatenate([stacked_high, stacked - stacked_high], 0).astype(BF16)
        inner = inner + dot(both, one_hot(inlet, (step * GROUP + j) * LANES))
        flow = flow_ref[:, :, lanes].reshape(leaving_ref.shape)
        leaving = leaving + dot_t(flow, one_hot(exits, 0))
    rows = inner.shape[0] // 2
    inner = inner[:rows] + inner[rows:]

    @pl.when(step == 0)
    def _():
        inner_ref[...] = inner
        leaving_ref[...] = leaving

    @pl.when(step > 0)
    def _():
        inner_ref[...] += inner
        leaving_ref[...] += leaving


def exchange_kernel(
    inner_ref, leaving_ref, outer_ref, own_ref, arrived_ref,
    out_box, in_box, back_box, home_box, send, recv, back_send, back_recv, flow_sem,
):
    count = out_box.shape[0]
    me = lax.axis_index("net")
    barrier = pltpu.get_barrier_semaphore()
    for i in range(1, count):
        peer = lax.rem(me + i, count)
        pl.semaphore_signal(barrier, inc=1, device_id={"net": peer}, device_id_type=MESH)
    rows = inner_ref.shape[0] - 8
    for k in range(count):
        out_box[k, 0:8, :] = inner_ref[pl.ds(k, 8, stride=rows // 8), :]
        out_box[k, 8:16, :] = inner_ref[rows : rows + 8, :]
    in_box[me] = out_box[me]
    pl.semaphore_wait(barrier, count - 1)

    def outward(peer, slot):
        return pltpu.make_async_remote_copy(
            src_ref=out_box.at[peer], dst_ref=in_box.at[slot], send_sem=send.at[peer], recv_sem=recv.at[slot],
            device_id={"net": peer}, device_id_type=MESH,
        )

    def homeward(peer, slot):
        return pltpu.make_async_remote_copy(
            src_ref=back_box.at[peer], dst_ref=home_box.at[slot], send_sem=back_send.at[peer],
            recv_sem=back_recv.at[slot], device_id={"net": peer}, device_id_type=MESH,
        )

    def flows(peer):
        return pltpu.make_async_remote_copy(
            src_ref=leaving_ref, dst_ref=arrived_ref, send_sem=flow_sem.at[0], recv_sem=flow_sem.at[1],
            device_id={"net": peer}, device_id_type=MESH,
        )

    for i in range(1, count):
        outward(lax.rem(me + i, count), me).start()

    @pl.when(me < count - 1)
    def _():
        flows(me + 1).start()

    place = lax.broadcasted_iota(jnp.int32, (8, LANES), 0)
    number = lax.broadcasted_iota(jnp.int32, (LANES, LANES), 0).astype(F32) + 1.0
    outer = jnp.zeros((8, LANES), F32)
    for p in reversed(range(count)):

        @pl.when(me != p)
        def _():
            outward(p, p).wait_recv()

        own = in_box[p, 0:8, :]
        if p < count - 1:
            picked = jnp.where(number == in_box[p, 12:13, :], 1.0, 0.0).astype(BF16)
            outer_high = outer.astype(BF16).astype(F32)
            both = jnp.concatenate([outer_high, outer - outer_high], 0).astype(BF16)
            both = dot(both, picked)
            taken = both[:8] + both[8:]
            own = own + taken * in_box[p, 8:9, :]
            for d in range(1, 4):
                later = jnp.where(place < 8 - 2 * d, pltpu.roll(taken, 8 - 2 * d, 0), 0.0)
                own = own + later * in_box[p, 8 + d : 9 + d, :]
        back_box[p, 0:8, :] = outer
        back_box[p, 8:16, :] = own

        @pl.when(me != p)
        def _():
            homeward(p, me).start()

        @pl.when(me == p)
        def _():
            home_box[p] = back_box[p]

        outer = own * in_box[p, 13:14, :] + jnp.where(place < 6, pltpu.roll(own, 6, 0), 0.0) * in_box[p, 14:15, :]

    for k in range(count):

        @pl.when(me != k)
        def _():
            homeward(k, k).wait_recv()

        outer_ref[pl.ds(k, 8, stride=rows // 8), :] = home_box[k, 0:8, :]
        own_ref[pl.ds(k, 8, stride=rows // 8), :] = home_box[k, 8:16, :]

    @pl.when(me > 0)
    def _():
        flows(me).wait_recv()

    @pl.when(me == 0)
    def _():
        arrived_ref[...] = jnp.zeros(arrived_ref.shape, F32)

    @pl.when(me < count - 1)
    def _():
        flows(me + 1).wait_send()

    for i in range(1, count):
        peer = lax.rem(me + i, count)
        outward(peer, me).wait_send()
        homeward(peer, me).wait_send()


def final_kernel(
    local_ref, gain_ref, flow_ref, lateral_ref, rough_ref, factor_ref, down_ref, inlet_ref, outer_ref, own_ref,
    arrived_ref, grad_ref, rough_grad_ref,
):
    step = pl.program_id(0)
    levels, members = flow_ref.shape[0], flow_ref.shape[1]
    steps = levels - 1
    outer_high, outer_low = split(outer_ref[...])
    outer = jnp.concatenate([outer_high, outer_low], 0)
    arrived = arrived_ref[...].reshape(levels, members, LANES)
    own = own_ref[...].reshape(steps, members, LANES)
    boundary = jnp.sum(
        jnp.sum(own * (-0.5 * arrived[1:] - 0.3 * arrived[:steps]), axis=0), axis=0, keepdims=True
    )
    boundary_high = boundary.astype(BF16).astype(F32)
    boundary = rows_of([boundary_high, boundary - boundary_high]).astype(BF16)
    inlet = inlet_ref[...]
    for j in range(GROUP):
        lanes = slice(j * LANES, (j + 1) * LANES)
        divisor = 0.8 * (rough_ref[j : j + 1, :] * factor_ref[j : j + 1, :]) + 0.5
        side = 1.0 / divisor
        scale = factor_ref[j : j + 1, :] / (divisor * divisor)
        slot = gain_ref[4:5, lanes]
        number = lax.broadcasted_iota(jnp.int32, (LANES, LANES), 0).astype(F32) + 1.0
        picked = jnp.where(number == slot, 1.0, 0.0).astype(BF16)
        taken = dot(outer, picked)
        rows = taken.shape[0] // 2
        taken = (taken[:rows] + taken[rows:]).reshape(steps, members, LANES)
        flow = flow_ref[:, :, lanes]
        inflow = dot_t(flow.reshape(levels * members, LANES), one_hot(down_ref[j : j + 1, :], 0))
        inflow = inflow.reshape(levels, members, LANES)
        total = jnp.zeros((members, LANES), F32)
        for t in range(steps):
            adjoint = local_ref[t, :, lanes]
            for d in range(steps - t):
                adjoint = adjoint + gain_ref[d : d + 1, lanes] * taken[t + d]
            grad_ref[t, :, lanes] = (side * adjoint).astype(BF16)
            held = flow[t].astype(F32) - lateral_ref[t, :, lanes].astype(F32)
            total = total + adjoint * (0.8 * held - 0.5 * inflow[t + 1] - 0.3 * inflow[t])
        placed = dot_t(boundary, one_hot(inlet, (step * GROUP + j) * LANES))
        rough_grad_ref[j : j + 1, :] = scale * (jnp.sum(total, axis=0, keepdims=True) + placed[0:1] + placed[1:2])


def sum_kernel(partial_ref, out_ref, out_box, in_box, send, recv):
    count = out_box.shape[0]
    me = lax.axis_index("mem")
    barrier = pltpu.get_barrier_semaphore()
    for i in range(1, count):
        peer = lax.rem(me + i, count)
        pl.semaphore_signal(barrier, inc=1, device_id={"mem": peer}, device_id_type=MESH)
    for k in range(count):
        out_box[k, 0:2, :] = partial_ref[2 * k : 2 * k + 2, :]
        out_box[k, 2:8, :] = jnp.zeros((6, LANES), F32)
    in_box[me] = out_box[me]
    pl.semaphore_wait(barrier, count - 1)

    def copy(peer, slot):
        return pltpu.make_async_remote_copy(
            src_ref=out_box.at[peer], dst_ref=in_box.at[slot], send_sem=send.at[peer], recv_sem=recv.at[slot],
            device_id={"mem": peer}, device_id_type=MESH,
        )

    for i in range(1, count):
        copy(lax.rem(me + i, count), me).start()
    for i in range(1, count):
        peer = lax.rem(me + i, count)
        copy(peer, peer).wait_recv()
    total = in_box[0]
    for k in range(1, count):
        total = total + in_box[k]
    out_ref[...] = total[0:2]
    for i in range(1, count):
        copy(lax.rem(me + i, count), me).wait_send()


def body(stored_reach_flows, lateral, cotangent, roughness, travel_factor, inverse_block_matrix, down_in_block, exit_slot, inlet_reach):
    steps, members, reaches = cotangent.shape
    levels = steps + 1
    blocks = reaches // LANES
    net, mem = lax.axis_size("net"), lax.axis_size("mem")
    rough = roughness.reshape(blocks, LANES)
    factor = travel_factor.reshape(blocks, LANES)
    down = down_in_block.reshape(blocks, LANES)
    exits = exit_slot.reshape(blocks, LANES)
    wide = GROUP * LANES

    def rows3(first):
        return pl.BlockSpec((first, members, wide), lambda g: (0, 0, g))

    per_block = pl.BlockSpec((GROUP, LANES), lambda g: (g, 0))

    def whole(*shape):
        return pl.BlockSpec(shape, lambda g: (0,) * len(shape))

    local, gain, inner, leaving = pl.pallas_call(
        local_kernel,
        grid=(blocks // GROUP,),
        in_specs=[
            rows3(steps), rows3(levels), per_block, per_block, per_block,
            pl.BlockSpec((GROUP, LANES, LANES), lambda g: (g, 0, 0)), whole(1, LANES),
        ],
        out_specs=[
            rows3(steps), pl.BlockSpec((8, wide), lambda g: (0, g)),
            whole(steps * members + 8, LANES), whole(levels * members, LANES),
        ],
        out_shape=[
            jax.ShapeDtypeStruct((steps, members, reaches), F32),
            jax.ShapeDtypeStruct((8, reaches), F32),
            jax.ShapeDtypeStruct((steps * members + 8, LANES), F32),
            jax.ShapeDtypeStruct((levels * members, LANES), F32),
        ],
        compiler_params=pltpu.CompilerParams(vmem_limit_bytes=40 << 20),
        name="local",
    )(cotangent, stored_reach_flows, rough, factor, exits, inverse_block_matrix, inlet_reach)

    vmem = pl.BlockSpec(memory_space=pltpu.VMEM)
    outer, own, arrived = pl.pallas_call(
        exchange_kernel,
        in_specs=[vmem] * 2,
        out_specs=[vmem] * 3,
        out_shape=[
            jax.ShapeDtypeStruct((steps * members, LANES), F32),
            jax.ShapeDtypeStruct((steps * members, LANES), F32),
            jax.ShapeDtypeStruct((levels * members, LANES), F32),
        ],
        scratch_shapes=[pltpu.VMEM((net, 16, LANES), F32)] * 4
        + [pltpu.SemaphoreType.DMA((net,))] * 4
        + [pltpu.SemaphoreType.DMA((2,))],
        compiler_params=pltpu.CompilerParams(collective_id=0, has_side_effects=True),
        name="exchange",
    )(inner, leaving)

    grad_lateral, partial = pl.pallas_call(
        final_kernel,
        grid=(blocks // GROUP,),
        in_specs=[
            rows3(steps), pl.BlockSpec((8, wide), lambda g: (0, g)), rows3(levels), rows3(steps), per_block, per_block,
            per_block, whole(1, LANES), whole(steps * members, LANES), whole(steps * members, LANES),
            whole(levels * members, LANES),
        ],
        out_specs=[rows3(steps), per_block],
        out_shape=[
            jax.ShapeDtypeStruct((steps, members, reaches), BF16),
            jax.ShapeDtypeStruct((blocks, LANES), F32),
        ],
        compiler_params=pltpu.CompilerParams(vmem_limit_bytes=40 << 20),
        name="final",
    )(local, gain, stored_reach_flows, lateral, rough, factor, down, inlet_reach, outer, own, arrived)

    grad_rough = pl.pallas_call(
        sum_kernel,
        in_specs=[vmem],
        out_specs=vmem,
        out_shape=jax.ShapeDtypeStruct((blocks // mem, LANES), F32),
        scratch_shapes=[pltpu.VMEM((mem, 8, LANES), F32)] * 2 + [pltpu.SemaphoreType.DMA((mem,))] * 2,
        compiler_params=pltpu.CompilerParams(collective_id=1, has_side_effects=True),
        name="rough_sum",
    )(partial)
    return grad_lateral, grad_rough.reshape(reaches // mem)


def solution(mesh):
    in_specs = (
        P(None, "mem", "net"),
        P(None, "mem", "net"),
        P(None, "mem", "net"),
        P("net"),
        P("net"),
        P("net", None, None),
        P("net"),
        P("net"),
        P("net", None),
    )
    out_specs = (P(None, "mem", "net"), P(("net", "mem")))
    return jax.shard_map(body, mesh=mesh, in_specs=in_specs, out_specs=out_specs, check_vma=False)
```

time: 1160 us -> 75.9 us (0.07)
  the two profiles are of different devices: /device:TPU:102 before, /device:TPU:1 now
where the time goes in v1:
time: 75.9 us; the launch traced here: 75.1 us
  Pallas kernels  58.5 us (77%)
  local copies, waits for them, and re-layouts  15.9 us (21%)
    pallas_call x1, Pallas kernels, body(): pl.pallas_call(exchange_kernel, in_specs=[vmem] * 2, out_specs=[vmem] * 3...  24.4 us
    pallas_call x1, Pallas kernels, body(): pl.pallas_call(local_kernel, grid=(blocks // GROUP,), in_specs=[rows3(ste...  20 us
    unnamed x39, local copies, waits for them, and re-layouts  15.9 us
    pallas_call x1, Pallas kernels, body(): pl.pallas_call(sum_kernel, in_specs=[vmem], out_specs=vmem, out_shape=jax...  10.7 us
    pallas_call x1, Pallas kernels, body(): pl.pallas_call(final_kernel, grid=(blocks // GROUP,), in_specs=[rows3(ste...  3.44 us

profile of v1, /device:TPU:1, one launch (start us, length us, event | category | flops | bytes accessed | tf_op | source)
XLA Modules:
  0.0 75.1 jit_solution(14067842585932277111)
XLA Ops:
  0.6 0.0 copy-start
  0.6 1.3 %copy-done = bf16[5,32,4096]{2,1,0:T(8,128)(2,1)S(1)} copy-done((bf16[5,32,4096]{2,1,0:T(8,128)(2,1)S(1)}, bf16[5,32,4096]{2,1,0:T(8,128)(2,1)}, u32[]{:S(2)}) %copy-start) | copy-done | bytes 1310744
  1.9 0.0 copy-start.2
  2.0 1.6 %copy-done.2 = f32[32,128,128]{2,1,0:T(8,128)S(1)} copy-done((f32[32,128,128]{2,1,0:T(8,128)S(1)}, f32[32,128,128]{2,1,0:T(8,128)}, u32[]{:S(2)}) %copy-start.2) | copy-done | bytes 2097176
  3.5 0.0 copy-start.3
  3.5 1.2 %copy-done.3 = bf16[4,32,4096]{2,1,0:T(8,128)(2,1)S(1)} copy-done((bf16[4,32,4096]{2,1,0:T(8,128)(2,1)S(1)}, bf16[4,32,4096]{2,1,0:T(8,128)(2,1)}, u32[]{:S(2)}) %copy-start.3) | copy-done | bytes 1048600
  4.8 0.7 copy-done.10
  5.5 0.0 copy-start.12
  5.5 0.7 copy-done.12
  6.2 0.0 copy-start.14
  6.2 0.7 copy-done.14
  6.9 0.0 copy-start.17
  6.9 0.7 copy-done.17
  7.6 20.0 %local.1 = (f32[4,32,4096]{2,1,0:T(8,128)S(1)}, f32[8,4096]{1,0:T(8,128)S(1)}, f32[136,128]{1,0:T(8,128)S(1)}, f32[160,128]{1,0:T(8,128)S(1)}) custom-call(bf16[4,32,4096]{2,1,0:T(8,128)(2,1)S(1)} %copy-done.3, bf16[5,32,4096]{2,1,0:T(8,128)(2,1)S(1)} %copy-done, f32[32,128]{1,0:T(8,128)S(1)} %bitcast.5, f32[32,128]{1,0:T(8,128)S(1)} %bitcast.7, ...), custom_call_target="tpu_custom_call" | custom-call | tf_op jit(solution)/shard_map/local/pallas_call | solution.py:299
  27.5 0.0 copy-start.5
  27.6 0.6 copy-done.5
  28.2 0.6 copy-done.7
  28.8 24.4 %exchange.1 = (f32[128,128]{1,0:T(8,128)}, f32[128,128]{1,0:T(8,128)}, f32[160,128]{1,0:T(8,128)}) custom-call(f32[136,128]{1,0:T(8,128)} %copy-done.7, f32[160,128]{1,0:T(8,128)} %copy-done.5), custom_call_target="tpu_custom_call" | custom-call | tf_op jit(solution)/shard_map/exchange/pallas_call | solution.py:321
  53.3 0.0 copy-done.1
  53.3 0.0 copy-done.11
  53.3 0.0 copy-start.4
  53.3 1.2 %copy-done.4 = bf16[4,32,4096]{2,1,0:T(8,128)(2,1)S(1)} copy-done((bf16[4,32,4096]{2,1,0:T(8,128)(2,1)S(1)}, bf16[4,32,4096]{2,1,0:T(8,128)(2,1)}, u32[]{:S(2)}) %copy-start.4) | copy-done | bytes 1048600
  54.5 0.9 %copy-done.6 = f32[160,128]{1,0:T(8,128)S(1)} copy-done((f32[160,128]{1,0:T(8,128)S(1)}, f32[160,128]{1,0:T(8,128)}, u32[]{:S(2)}) %copy-start.6) | copy-done | bytes 81944
  55.4 0.8 %copy-done.8 = f32[128,128]{1,0:T(8,128)S(1)} copy-done((f32[128,128]{1,0:T(8,128)S(1)}, f32[128,128]{1,0:T(8,128)}, u32[]{:S(2)}) %copy-start.8) | copy-done | bytes 65560
  56.2 0.8 %copy-done.9 = f32[128,128]{1,0:T(8,128)S(1)} copy-done((f32[128,128]{1,0:T(8,128)S(1)}, f32[128,128]{1,0:T(8,128)}, u32[]{:S(2)}) %copy-start.9) | copy-done | bytes 65560
  57.1 0.7 copy-done.13
  57.8 0.7 copy-done.15
  58.5 0.7 copy-done.18
  59.2 3.4 %final.1 = (bf16[4,32,4096]{2,1,0:T(8,128)(2,1)}, f32[32,128]{1,0:T(8,128)S(1)}) custom-call(f32[4,32,4096]{2,1,0:T(8,128)S(1)} %get-tuple-element.11.local_ref, f32[8,4096]{1,0:T(8,128)S(1)} %get-tuple-element.12.gain_ref, bf16[5,32,4096]{2,1,0:T(8,128)(2,1)S(1)} %copy-done.1, bf16[4,32,4096]{2,1,0:T(8,128)(2,1)S(1)} %copy-done.4, f32[32,128]{1,0:T(8,128)S(1)} %bitcast.6, ...), custom_call_target="tpu_custom_call" | custom-call | tf_op jit(solution)/shard_map/final/pallas_call | solution.py:337
  62.6 0.6 copy-done.16
  63.2 10.7 %rough_sum.1 = f32[2,128]{1,0:T(2,128)} custom-call(f32[32,128]{1,0:T(8,128)} %copy-done.16), custom_call_target="tpu_custom_call" | custom-call | tf_op jit(solution)/shard_map/rough_sum/pallas_call | solution.py:354
  73.9 1.2 %copy.12 = f32[256]{0:T(256)} copy(f32[256]{0:T(256)} %bitcast.11) | data formatting | bytes 2048
  (11 shorter events, 0.0 us)
Async XLA Ops:
  0.6 1.3 %copy-start = (bf16[5,32,4096]{2,1,0:T(8,128)(2,1)S(1)}, bf16[5,32,4096]{2,1,0:T(8,128)(2,1)}, u32[]{:S(2)}) copy-start(bf16[5,32,4096]{2,1,0:T(8,128)(2,1)} %flow_ref.3) | copy-start | bytes 3932164
  1.9 1.6 %copy-start.2 = (f32[32,128,128]{2,1,0:T(8,128)S(1)}, f32[32,128,128]{2,1,0:T(8,128)}, u32[]{:S(2)}) copy-start(f32[32,128,128]{2,1,0:T(8,128)} %matrix_ref.1) | copy-start | bytes 6291460
  3.5 1.2 %copy-start.3 = (bf16[4,32,4096]{2,1,0:T(8,128)(2,1)S(1)}, bf16[4,32,4096]{2,1,0:T(8,128)(2,1)}, u32[]{:S(2)}) copy-start(bf16[4,32,4096]{2,1,0:T(8,128)(2,1)} %cot_ref.1) | copy-start | bytes 3145732
  4.8 0.7 copy-start.10
  5.5 0.7 copy-start.12
  6.2 0.7 copy-start.14
  6.9 0.7 copy-start.17
  7.6 45.7 %copy-start.1 = (bf16[5,32,4096]{2,1,0:T(8,128)(2,1)S(1)}, bf16[5,32,4096]{2,1,0:T(8,128)(2,1)}, u32[]{:S(2)}) copy-start(bf16[5,32,4096]{2,1,0:T(8,128)(2,1)} %flow_ref.3) | copy-start | bytes 3932164
  7.6 45.7 %copy-start.11 = (f32[4096]{0:T(1024)S(1)}, f32[4096]{0:T(1024)}, u32[]{:S(2)}) copy-start(f32[4096]{0:T(1024)} %param.12) | copy-start | bytes 49156
  27.5 0.6 copy-start.5
  28.2 0.6 copy-start.7
  53.3 1.2 %copy-start.4 = (bf16[4,32,4096]{2,1,0:T(8,128)(2,1)S(1)}, bf16[4,32,4096]{2,1,0:T(8,128)(2,1)}, u32[]{:S(2)}) copy-start(bf16[4,32,4096]{2,1,0:T(8,128)(2,1)} %lateral_ref.1) | copy-start | bytes 3145732
  54.5 0.9 %copy-start.6 = (f32[160,128]{1,0:T(8,128)S(1)}, f32[160,128]{1,0:T(8,128)}, u32[]{:S(2)}) copy-start(f32[160,128]{1,0:T(8,128)} %get-tuple-element.17.arrived_ref) | copy-start | bytes 245764
  55.4 0.8 %copy-start.8 = (f32[128,128]{1,0:T(8,128)S(1)}, f32[128,128]{1,0:T(8,128)}, u32[]{:S(2)}) copy-start(f32[128,128]{1,0:T(8,128)} %get-tuple-element.15.outer_ref) | copy-start | bytes 196612
  56.2 0.8 %copy-start.9 = (f32[128,128]{1,0:T(8,128)S(1)}, f32[128,128]{1,0:T(8,128)}, u32[]{:S(2)}) copy-start(f32[128,128]{1,0:T(8,128)} %get-tuple-element.16.own_ref) | copy-start | bytes 196612
  57.1 0.7 copy-start.13
  57.8 0.7 copy-start.15
  58.5 0.7 copy-start.18
  62.6 0.6 copy-start.16

commit v2 on v0

v2 whole, which is shorter than its diff:
```python
import jax
import jax.numpy as jnp
from jax import lax
from jax.experimental import pallas as pl
from jax.experimental.pallas import tpu as pltpu
from jax.sharding import PartitionSpec as P

F32, BF16 = jnp.float32, jnp.bfloat16
LANES = 128
GROUP = 8
WIDE = GROUP * LANES
MESH = pl.DeviceIdType.MESH


def dot(a, b):
    return lax.dot_general(a, b, (((1,), (0,)), ((), ())), preferred_element_type=F32)


def dot_t(a, b):
    return lax.dot_general(a, b, (((1,), (1,)), ((), ())), preferred_element_type=F32)


def split(value):
    high = value.astype(BF16)
    return high, (value - high.astype(F32)).astype(BF16)


def stack_split(value):
    high = value.astype(BF16).astype(F32)
    return jnp.concatenate([high, value - high], 0).astype(BF16)


def halves(value):
    rows = value.shape[0] // 2
    return value[:rows] + value[rows:]


def rows_of(rows):
    place = lax.broadcasted_iota(jnp.int32, (8, LANES), 0)
    out = jnp.zeros((8, LANES), F32)
    for i, row in enumerate(rows):
        out = jnp.where(place == i, jnp.broadcast_to(row, (8, LANES)), out)
    return out


def one_hot(row, start):
    place = lax.broadcasted_iota(jnp.int32, (LANES, LANES), 0) + start
    return jnp.where(place == row, 1.0, 0.0).astype(BF16)


def pick(slot):
    number = lax.broadcasted_iota(jnp.int32, (LANES, LANES), 0).astype(F32) + 1.0
    return jnp.where(number == slot, 1.0, 0.0).astype(BF16)


def kernel(
    cot_hbm, flow_hbm, lateral_hbm, matrix_hbm, rough_hbm, factor_hbm, exits_hbm, down_hbm, inlet_hbm,
    grad, rough_out,
    cot, flow, lateral, matrix, rough, factor, exits, down, inlet,
    table, local, gain, term, inner, leaving, arrived, edge, outer,
    out_box, in_box, back_box, home_box, partial, sum_out, sum_in,
    small_sem, matrix_sem, cot_sem, flow_sem, lateral_sem,
    send, recv, back_send, back_recv, cross_sem, sum_send, sum_recv,
):
    net, mem = out_box.shape[0], sum_out.shape[0]
    steps, members, reaches = cot.shape
    levels = steps + 1
    rows = steps * members
    stride = rows // 8
    groups = reaches // WIDE
    me, you = lax.axis_index("net"), lax.axis_index("mem")

    barrier = pltpu.get_barrier_semaphore()
    for i in range(1, net):
        pl.semaphore_signal(barrier, inc=1, device_id={"net": lax.rem(me + i, net)}, device_id_type=MESH)
    for i in range(1, mem):
        pl.semaphore_signal(barrier, inc=1, device_id={"mem": lax.rem(you + i, mem)}, device_id_type=MESH)

    smalls = [
        pltpu.make_async_copy(a, b, small_sem.at[i])
        for i, (a, b) in enumerate(
            [(rough_hbm, rough), (factor_hbm, factor), (exits_hbm, exits), (inlet_hbm, inlet), (down_hbm, down)]
        )
    ]

    def lanes_of(g):
        return pl.ds(pl.multiple_of(g * WIDE, WIDE), WIDE)

    def matrix_copy(g):
        block = pl.ds(g * GROUP, GROUP)
        return pltpu.make_async_copy(matrix_hbm.at[block], matrix.at[block], matrix_sem.at[g])

    def wide_copy(source, target, sem, g):
        return pltpu.make_async_copy(source.at[:, :, lanes_of(g)], target.at[:, :, lanes_of(g)], sem.at[g])

    for copy in smalls[:4]:
        copy.start()
    for g in range(groups):
        matrix_copy(g).start()
        wide_copy(cot_hbm, cot, cot_sem, g).start()
    smalls[4].start()
    for g in range(groups):
        wide_copy(flow_hbm, flow, flow_sem, g).start()
        wide_copy(lateral_hbm, lateral, lateral_sem, g).start()

    for copy in smalls[:4]:
        copy.wait()
    travel = rough[...] * factor[...]
    divisor = 0.8 * travel + 0.5
    numer_new = 0.5 - 0.2 * travel
    numer_old = 0.5 + 0.2 * travel
    ratio = numer_old / numer_new
    side = 1.0 / divisor
    table[0] = (0.8 * travel - 0.5) / divisor + ratio
    table[1] = ratio
    table[2] = numer_new / divisor
    table[3] = numer_old / divisor
    table[4] = side
    table[5] = factor[...] / (divisor * divisor)
    inner[...] = jnp.zeros(inner.shape, F32)
    leaving[...] = jnp.zeros(leaving.shape, F32)

    def eight(ref, g):
        return ref[pl.ds(pl.multiple_of(g * GROUP, GROUP), GROUP), :]

    def solve(g, carried):
        matrix_copy(g).wait()
        wide_copy(cot_hbm, cot, cot_sem, g).wait()
        lanes = [pl.ds(pl.multiple_of(g * WIDE + j * LANES, LANES), LANES) for j in range(GROUP)]
        carry, ratio, weight_new, weight_old = (eight(table.at[k], g) for k in range(4))
        exit_rows = eight(exits, g)
        opened = jnp.where(exit_rows >= 0, 1.0, 0.0)
        numbered = jnp.where(exit_rows >= 0, exit_rows + 1, 0).astype(F32)
        weights = []
        slots = []
        for j in range(GROUP):
            block = matrix[g * GROUP + j]
            weights.append(split(block))
            pattern = jnp.where(block != 0.0, 1.0, 0.0).astype(BF16)
            slots.append(dot(jnp.broadcast_to(numbered[j : j + 1], (8, LANES)).astype(BF16), pattern)[0:1])
        adjoint = [None] * GROUP
        found = [[None] * steps for _ in range(GROUP)]
        gains = [[] for _ in range(GROUP)]
        for t in reversed(range(steps)):
            for j in range(GROUP):
                high, low = weights[j]
                start = cot[t, :, lanes[j]].astype(F32)
                if t == steps - 1:
                    x = jnp.concatenate([start, jnp.broadcast_to(opened[j : j + 1], (8, LANES))], 0).astype(BF16)
                    value = dot(x, high) + dot(x, low)
                else:
                    x = jnp.concatenate([start, jnp.zeros((8, LANES), F32)], 0) + adjoint[j] * carry[j : j + 1]
                    x_high, x_low = split(x)
                    value = dot(x_high, high) + dot(x_low, high) + dot(x_high, low) - adjoint[j] * ratio[j : j + 1]
                adjoint[j] = value
                found[j][t] = value[:members]
                local[t, :, lanes[j]] = value[:members]
                gains[j].append(value[members : members + 1])
        total = jnp.zeros(inner.shape, F32)
        for j in range(GROUP):
            facts = rows_of(gains[j] + [slots[j], weight_new[j : j + 1], weight_old[j : j + 1]])
            gain[:, lanes[j]] = facts
            both = stack_split(jnp.concatenate(found[j] + [facts], 0))
            total = total + dot(both, one_hot(inlet[...], (g * GROUP + j) * LANES))
        inner[...] += total
        return carried

    lax.fori_loop(0, groups, solve, 0)

    inside = halves(inner[...])
    facts = inside[rows:]
    inside = inside[:rows]
    weight_new, weight_old = facts[5:6], facts[6:7]
    edge[...] = weight_new * inside + weight_old * jnp.concatenate(
        [inside[members:], jnp.zeros((members, LANES), F32)], 0
    )
    passed = [weight_new * facts[0:1]] + [weight_new * facts[d : d + 1] + weight_old * facts[d - 1 : d] for d in range(1, steps)]
    message = rows_of(passed + [facts[4:5]])
    for k in range(net):
        out_box[k, 0:8, :] = edge[pl.ds(k, 8, stride=stride), :]
        out_box[k, 8:16, :] = message
    in_box[me] = out_box[me]

    def outward(peer, slot):
        return pltpu.make_async_remote_copy(
            src_ref=out_box.at[peer], dst_ref=in_box.at[slot], send_sem=send.at[peer], recv_sem=recv.at[slot],
            device_id={"net": peer}, device_id_type=MESH,
        )

    def homeward(peer, slot):
        return pltpu.make_async_remote_copy(
            src_ref=back_box.at[peer], dst_ref=home_box.at[slot], send_sem=back_send.at[peer],
            recv_sem=back_recv.at[slot], device_id={"net": peer}, device_id_type=MESH,
        )

    def across(peer):
        return pltpu.make_async_remote_copy(
            src_ref=leaving, dst_ref=arrived, send_sem=cross_sem.at[0], recv_sem=cross_sem.at[1],
            device_id={"net": peer}, device_id_type=MESH,
        )

    def sums(peer, slot):
        return pltpu.make_async_remote_copy(
            src_ref=sum_out.at[peer], dst_ref=sum_in.at[slot], send_sem=sum_send.at[peer], recv_sem=sum_recv.at[slot],
            device_id={"mem": peer}, device_id_type=MESH,
        )

    if net + mem > 2:
        pl.semaphore_wait(barrier, net + mem - 2)

    @pl.when(me > 0)
    def _():
        for i in range(1, net):
            outward(lax.rem(me + i, net), me).start()

    smalls[4].wait()

    def inflows(g, carried):
        wide_copy(flow_hbm, flow, flow_sem, g).wait()
        wide_copy(lateral_hbm, lateral, lateral_sem, g).wait()
        down_rows, exit_rows = eight(down, g), eight(exits, g)
        total = jnp.zeros(leaving.shape, F32)
        for j in range(GROUP):
            lanes = pl.ds(pl.multiple_of(g * WIDE + j * LANES, LANES), LANES)
            here = flow[:, :, lanes]
            flat = here.reshape(levels * members, LANES)
            inflow = dot_t(flat, one_hot(down_rows[j : j + 1], 0)).reshape(levels, members, LANES)
            total = total + dot_t(flat, one_hot(exit_rows[j : j + 1], 0))
            held = here[:steps].astype(F32) - lateral[:, :, lanes].astype(F32)
            term[:, :, lanes] = 0.8 * held - 0.5 * inflow[1:] - 0.3 * inflow[:steps]
        leaving[...] += total
        return carried

    lax.fori_loop(0, groups, inflows, 0)

    @pl.when(me < net - 1)
    def _():
        across(me + 1).start()

    place = lax.broadcasted_iota(jnp.int32, (8, LANES), 0)
    state = None
    for p in reversed(range(1, net)):

        @pl.when(me != p)
        def _():
            outward(p, p).wait_recv()

        own = in_box[p, 0:8, :]
        if state is not None:
            both = halves(dot(stack_split(state), pick(in_box[p, 12:13, :])))
            own = own + both * in_box[p, 8:9, :]
            for d in range(1, steps):
                later = jnp.where(place < 8 - 2 * d, pltpu.roll(both, 8 - 2 * d, 0), 0.0)
                own = own + later * in_box[p, 8 + d : 9 + d, :]
        state = own
        back_box[p - 1] = state

        @pl.when(me != p - 1)
        def _():
            homeward(p - 1, me).start()

        @pl.when(me == p - 1)
        def _():
            home_box[p - 1] = back_box[p - 1]

    @pl.when(me == net - 1)
    def _():
        outer[...] = jnp.zeros(outer.shape, F32)

    @pl.when(me < net - 1)
    def _():
        for k in range(net):

            @pl.when(me != k)
            def _():
                homeward(k, k).wait_recv()

            outer[pl.ds(k, 8, stride=stride), :] = home_box[k]

    both = stack_split(outer[...])

    def taken_at(slot):
        return halves(dot(both, pick(slot))).reshape(steps, members, LANES)

    def finish(g, carried):
        side, scale = eight(table.at[4], g), eight(table.at[5], g)
        out = []
        for j in range(GROUP):
            lanes = pl.ds(pl.multiple_of(g * WIDE + j * LANES, LANES), LANES)
            facts = gain[:, lanes]
            taken = taken_at(facts[4:5])
            total = jnp.zeros((members, LANES), F32)
            for t in range(steps):
                adjoint = local[t, :, lanes]
                for d in range(steps - t):
                    adjoint = adjoint + facts[d : d + 1] * taken[t + d]
                grad[t, :, lanes] = (side[j : j + 1] * adjoint).astype(BF16)
                total = total + adjoint * term[t, :, lanes]
            out.append(jnp.sum(total, axis=0, keepdims=True))
        partial[pl.ds(pl.multiple_of(g * GROUP, GROUP), GROUP), :] = rows_of(out)
        return carried

    lax.fori_loop(0, groups, finish, 0)

    @pl.when(me > 0)
    def _():
        across(me).wait_recv()

    @pl.when(me == 0)
    def _():
        arrived[...] = jnp.zeros(arrived.shape, F32)

    came = arrived[...].reshape(levels, members, LANES)
    came = -0.5 * came[1:] - 0.3 * came[:steps]
    taken = taken_at(facts[4:5])
    total = jnp.zeros((members, LANES), F32)
    for t in range(steps):
        adjoint = inside[t * members : (t + 1) * members]
        for d in range(steps - t):
            adjoint = adjoint + facts[d : d + 1] * taken[t + d]
        total = total + adjoint * came[t]
    total = jnp.sum(total, axis=0, keepdims=True)
    high = total.astype(BF16).astype(F32)
    total = rows_of([high, total - high]).astype(BF16)
    within = lax.broadcasted_iota(jnp.int32, (LANES, LANES), 0)
    lane = lax.broadcasted_iota(jnp.int32, (8, LANES), 1)
    for g in range(groups):
        out = []
        for h in range(GROUP // 4):
            first = (g * GROUP + h * 4) * LANES
            near = jnp.where(within // 32 * LANES + within % 32 + first == inlet[...], 1.0, 0.0).astype(BF16)
            placed = dot_t(total, near)
            placed = placed + pltpu.roll(placed, 7, 0)
            for i in range(4):
                shifted = placed if i == 0 else pltpu.roll(placed, LANES - 32 * i, 1)
                out.append(jnp.where(lane < 32, shifted, 0.0)[0:1])
        here = pl.ds(g * GROUP, GROUP)
        partial[here, :] = (partial[here, :] + rows_of(out)) * table[5, here, :]

    for k in range(mem):
        sum_out[k] = jnp.zeros((8, LANES), F32)
        sum_out[k, 0:2, :] = partial[2 * k : 2 * k + 2, :]
    sum_in[you] = sum_out[you]
    for i in range(1, mem):
        sums(lax.rem(you + i, mem), you).start()
    for i in range(1, mem):
        peer = lax.rem(you + i, mem)
        sums(peer, peer).wait_recv()
    total = sum_in[0]
    for k in range(1, mem):
        total = total + sum_in[k]
    rough_out[...] = total[0:2]

    for i in range(1, mem):
        sums(lax.rem(you + i, mem), you).wait_send()

    @pl.when(me > 0)
    def _():
        for i in range(1, net):
            outward(lax.rem(me + i, net), me).wait_send()

    @pl.when(me < net - 1)
    def _():
        across(me + 1).wait_send()

    for p in range(net - 1):

        @pl.when(me != p)
        def _():
            homeward(p, me).wait_send()


def body(stored_reach_flows, lateral, cotangent, roughness, travel_factor, inverse_block_matrix, down_in_block, exit_slot, inlet_reach):
    steps, members, reaches = cotangent.shape
    levels = steps + 1
    blocks = reaches // LANES
    groups = reaches // WIDE
    net, mem = lax.axis_size("net"), lax.axis_size("mem")

    def blocked(value):
        return value.reshape(blocks, LANES)

    anywhere = pl.BlockSpec(memory_space=pltpu.HBM)
    vmem = pl.BlockSpec(memory_space=pltpu.VMEM)
    dma = pltpu.SemaphoreType.DMA
    shaped = pltpu.VMEM
    per_block = [shaped((blocks, LANES), F32)] * 2 + [shaped((blocks, LANES), jnp.int32)]
    grad_lateral, grad_rough = pl.pallas_call(
        kernel,
        in_specs=[anywhere] * 9,
        out_specs=[vmem, vmem],
        out_shape=[
            jax.ShapeDtypeStruct((steps, members, reaches), BF16),
            jax.ShapeDtypeStruct((2, LANES), F32),
        ],
        scratch_shapes=[
            shaped((steps, members, reaches), BF16),
            shaped((levels, members, reaches), BF16),
            shaped((steps, members, reaches), BF16),
            shaped((blocks, LANES, LANES), F32),
            *per_block,
            shaped((blocks, LANES), jnp.int32),
            shaped((1, LANES), jnp.int32),
            shaped((6, blocks, LANES), F32),
            shaped((steps, members, reaches), F32),
            shaped((8, reaches), F32),
            shaped((steps, members, reaches), F32),
            shaped((2 * (steps * members + 8), LANES), F32),
            shaped((levels * members, LANES), F32),
            shaped((levels * members, LANES), F32),
            shaped((steps * members, LANES), F32),
            shaped((steps * members, LANES), F32),
            shaped((net, 16, LANES), F32),
            shaped((net, 16, LANES), F32),
            shaped((net, 8, LANES), F32),
            shaped((net, 8, LANES), F32),
            shaped((blocks, LANES), F32),
            shaped((mem, 8, LANES), F32),
            shaped((mem, 8, LANES), F32),
            dma((5,)), dma((groups,)), dma((groups,)), dma((groups,)), dma((groups,)),
            dma((net,)), dma((net,)), dma((net,)), dma((net,)), dma((2,)), dma((mem,)), dma((mem,)),
        ],
        compiler_params=pltpu.CompilerParams(collective_id=0, has_side_effects=True, vmem_limit_bytes=56 << 20),
        name="adjoint",
    )(
        cotangent, stored_reach_flows, lateral, inverse_block_matrix, blocked(roughness), blocked(travel_factor),
        blocked(exit_slot), blocked(down_in_block), inlet_reach,
    )
    return grad_lateral, grad_rough.reshape(2 * LANES)


def solution(mesh):
    in_specs = (
        P(None, "mem", "net"),
        P(None, "mem", "net"),
        P(None, "mem", "net"),
        P("net"),
        P("net"),
        P("net", None, None),
        P("net"),
        P("net"),
        P("net", None),
    )
    out_specs = (P(None, "mem", "net"), P(("net", "mem")))
    return jax.shard_map(body, mesh=mesh, in_specs=in_specs, out_specs=out_specs, check_vma=False)
```

time: 1160 us -> 39.1 us (0.03)
  the two profiles are of different devices: /device:TPU:102 before, /device:TPU:1 now
where the time goes in v2:
time: 39.1 us; the launch traced here: 38.9 us
  Pallas kernels  35.4 us (91%)
  local copies, waits for them, and re-layouts  2.86 us (7%)
  between operations  0.65 us (2%)
    pallas_call x1, Pallas kernels, body(): pl.pallas_call(kernel, in_specs=[anywhere] * 9, out_specs=[vmem, vmem], o...  35.4 us
    unnamed x4, local copies, waits for them, and re-layouts  2.86 us

profile of v2, /device:TPU:1, one launch (start us, length us, event | category | flops | bytes accessed | tf_op | source)
XLA Modules:
  0.0 38.9 jit_solution(17138399237656531484)
XLA Ops:
  0.6 35.4 %adjoint.1 = (bf16[4,32,4096]{2,1,0:T(8,128)(2,1)}, f32[2,128]{1,0:T(2,128)}) custom-call(bf16[4,32,4096]{2,1,0:T(8,128)(2,1)} %cot_hbm.1, bf16[5,32,4096]{2,1,0:T(8,128)(2,1)} %flow_hbm.1, bf16[4,32,4096]{2,1,0:T(8,128)(2,1)} %lateral_hbm.1, f32[32,128,128]{2,1,0:T(8,128)} %matrix_hbm.1, f32[32,128]{1,0:T(8,128)} %bitcast.5, f32[32,128]{1,0:T(8,128)} %bitcast.6, ...), custom_call_target="tpu_custom_call" | custom-call | tf_op jit(solution)/shard_map/adjoint/pallas_call | solution.py:388
  36.1 0.0 copy-start
  36.1 2.3 %copy.13 = bf16[4,32,4096]{2,1,0:T(8,128)(2,1)} copy(bf16[4,32,4096]{2,1,0:T(8,128)(2,1)} %get-tuple-element.8) | data formatting | bytes 2097152
  38.4 0.0 copy-done
  38.4 0.6 %copy.14 = f32[256]{0:T(256)} copy(f32[256]{0:T(256)S(1)} %bitcast.9) | data formatting | bytes 2048
Async XLA Ops:
  36.1 2.3 %copy-start = (f32[2,128]{1,0:T(2,128)S(1)}, f32[2,128]{1,0:T(2,128)}, u32[]{:S(2)}) copy-start(f32[2,128]{1,0:T(2,128)} %get-tuple-element.5) | copy-start | bytes 3076

commit v3 on v2

--- a/solution.py
+++ b/solution.py
@@ -57,7 +57,7 @@
     cot_hbm, flow_hbm, lateral_hbm, matrix_hbm, rough_hbm, factor_hbm, exits_hbm, down_hbm, inlet_hbm,
     grad, rough_out,
     cot, flow, lateral, matrix, rough, factor, exits, down, inlet,
-    table, local, gain, term, inner, leaving, arrived, edge, outer,
+    table, local, gain, term, taken, inner, leaving, arrived, edge, outer,
     out_box, in_box, back_box, home_box, partial, sum_out, sum_in,
     small_sem, matrix_sem, cot_sem, flow_sem, lateral_sem,
     send, recv, back_send, back_recv, cross_sem, sum_send, sum_recv,
@@ -70,12 +70,6 @@
     groups = reaches // WIDE
     me, you = lax.axis_index("net"), lax.axis_index("mem")
 
-    barrier = pltpu.get_barrier_semaphore()
-    for i in range(1, net):
-        pl.semaphore_signal(barrier, inc=1, device_id={"net": lax.rem(me + i, net)}, device_id_type=MESH)
-    for i in range(1, mem):
-        pl.semaphore_signal(barrier, inc=1, device_id={"mem": lax.rem(you + i, mem)}, device_id_type=MESH)
-
     smalls = [
         pltpu.make_async_copy(a, b, small_sem.at[i])
         for i, (a, b) in enumerate(
@@ -102,6 +96,12 @@
     for g in range(groups):
         wide_copy(flow_hbm, flow, flow_sem, g).start()
         wide_copy(lateral_hbm, lateral, lateral_sem, g).start()
+
+    barrier = pltpu.get_barrier_semaphore()
+    for i in range(1, net):
+        pl.semaphore_signal(barrier, inc=1, device_id={"net": lax.rem(me + i, net)}, device_id_type=MESH)
+    for i in range(1, mem):
+        pl.semaphore_signal(barrier, inc=1, device_id={"mem": lax.rem(you + i, mem)}, device_id_type=MESH)
 
     for copy in smalls[:4]:
         copy.wait()
@@ -131,11 +131,13 @@
         exit_rows = eight(exits, g)
         opened = jnp.where(exit_rows >= 0, 1.0, 0.0)
         numbered = jnp.where(exit_rows >= 0, exit_rows + 1, 0).astype(F32)
-        weights = []
+        weights, twice, whole = [], [], []
         slots = []
         for j in range(GROUP):
             block = matrix[g * GROUP + j]
             weights.append(split(block))
+            twice.append(jnp.concatenate([weights[-1][0]] * 2, 0))
+            whole.append(jnp.concatenate(weights[-1], 0))
             pattern = jnp.where(block != 0.0, 1.0, 0.0).astype(BF16)
             slots.append(dot(jnp.broadcast_to(numbered[j : j + 1], (8, LANES)).astype(BF16), pattern)[0:1])
         adjoint = [None] * GROUP
@@ -147,27 +149,29 @@
                 start = cot[t, :, lanes[j]].astype(F32)
                 if t == steps - 1:
                     x = jnp.concatenate([start, jnp.broadcast_to(opened[j : j + 1], (8, LANES))], 0).astype(BF16)
-                    value = dot(x, high) + dot(x, low)
+                    value = dot(jnp.concatenate([x, x], 1), whole[j])
                 else:
                     x = jnp.concatenate([start, jnp.zeros((8, LANES), F32)], 0) + adjoint[j] * carry[j : j + 1]
                     x_high, x_low = split(x)
-                    value = dot(x_high, high) + dot(x_low, high) + dot(x_high, low) - adjoint[j] * ratio[j : j + 1]
+                    value = dot(jnp.concatenate([x_high, x_low], 1), twice[j]) + dot(x_high, low) - adjoint[j] * ratio[j : j + 1]
                 adjoint[j] = value
                 found[j][t] = value[:members]
                 local[t, :, lanes[j]] = value[:members]
                 gains[j].append(value[members : members + 1])
-        total = jnp.zeros(inner.shape, F32)
+        pieces, marks = [], []
         for j in range(GROUP):
             facts = rows_of(gains[j] + [slots[j], weight_new[j : j + 1], weight_old[j : j + 1]])
             gain[:, lanes[j]] = facts
-            both = stack_split(jnp.concatenate(found[j] + [facts], 0))
-            total = total + dot(both, one_hot(inlet[...], (g * GROUP + j) * LANES))
-        inner[...] += total
+            both = split(jnp.concatenate(found[j] + [facts], 0))
+            mark = one_hot(inlet[...], (g * GROUP + j) * LANES)
+            pieces += both
+            marks += [mark, mark]
+        inner[...] += dot(jnp.concatenate(pieces, 1), jnp.concatenate(marks, 0))
         return carried
 
     lax.fori_loop(0, groups, solve, 0)
 
-    inside = halves(inner[...])
+    inside = inner[...]
     facts = inside[rows:]
     inside = inside[:rows]
     weight_new, weight_old = facts[5:6], facts[6:7]
@@ -181,6 +185,12 @@
         out_box[k, 8:16, :] = message
     in_box[me] = out_box[me]
 
+    far = sorted(range(net), key=lambda i: -(2 * (i % 2) + min(i // 2, net // 2 - i // 2)))
+    high, low = me // 2, lax.rem(me, 2)
+
+    def peer_at(i):
+        return 2 * lax.rem(high + i // 2, net // 2) + lax.rem(low + i % 2, 2)
+
     def outward(peer, slot):
         return pltpu.make_async_remote_copy(
             src_ref=out_box.at[peer], dst_ref=in_box.at[slot], send_sem=send.at[peer], recv_sem=recv.at[slot],
@@ -210,8 +220,8 @@
 
     @pl.when(me > 0)
     def _():
-        for i in range(1, net):
-            outward(lax.rem(me + i, net), me).start()
+        for i in far[:-1]:
+            outward(peer_at(i), me).start()
 
     smalls[4].wait()
 
@@ -219,16 +229,25 @@
         wide_copy(flow_hbm, flow, flow_sem, g).wait()
         wide_copy(lateral_hbm, lateral, lateral_sem, g).wait()
         down_rows, exit_rows = eight(down, g), eight(exits, g)
-        total = jnp.zeros(leaving.shape, F32)
+        marks, out = [], []
         for j in range(GROUP):
             lanes = pl.ds(pl.multiple_of(g * WIDE + j * LANES, LANES), LANES)
             here = flow[:, :, lanes]
             flat = here.reshape(levels * members, LANES)
             inflow = dot_t(flat, one_hot(down_rows[j : j + 1], 0)).reshape(levels, members, LANES)
-            total = total + dot_t(flat, one_hot(exit_rows[j : j + 1], 0))
+            marks.append(one_hot(exit_rows[j : j + 1], 0))
+            facts = gain[:, lanes]
             held = here[:steps].astype(F32) - lateral[:, :, lanes].astype(F32)
-            term[:, :, lanes] = 0.8 * held - 0.5 * inflow[1:] - 0.3 * inflow[:steps]
-        leaving[...] += total
+            terms = 0.8 * held - 0.5 * inflow[1:] - 0.3 * inflow[:steps]
+            out.append(jnp.sum(jnp.sum(terms * local[:, :, lanes], axis=0), axis=0, keepdims=True))
+            for t in range(steps):
+                weighted = terms[t] * facts[0:1]
+                for d in range(1, t + 1):
+                    weighted = weighted + terms[t - d] * facts[d : d + 1]
+                term[t, :, lanes] = weighted
+        partial[pl.ds(pl.multiple_of(g * GROUP, GROUP), GROUP), :] = rows_of(out)
+        flat = flow[:, :, lanes_of(g)].reshape(levels * members, WIDE)
+        leaving[...] += dot_t(flat, jnp.concatenate(marks, 1))
         return carried
 
     lax.fori_loop(0, groups, inflows, 0)
@@ -237,31 +256,50 @@
     def _():
         across(me + 1).start()
 
-    place = lax.broadcasted_iota(jnp.int32, (8, LANES), 0)
-    state = None
-    for p in reversed(range(1, net)):
+    for p in range(1, net):
 
         @pl.when(me != p)
         def _():
             outward(p, p).wait_recv()
 
-        own = in_box[p, 0:8, :]
-        if state is not None:
-            both = halves(dot(stack_split(state), pick(in_box[p, 12:13, :])))
-            own = own + both * in_box[p, 8:9, :]
-            for d in range(1, steps):
-                later = jnp.where(place < 8 - 2 * d, pltpu.roll(both, 8 - 2 * d, 0), 0.0)
-                own = own + later * in_box[p, 8 + d : 9 + d, :]
-        state = own
+    place = lax.broadcasted_iota(jnp.int32, (8, LANES), 0)
+    state = in_box[net - 1, 0:8, :]
+    back_box[net - 2] = state
+    for p in reversed(range(1, net - 1)):
+        slot = jnp.maximum(in_box[p, 12:13, :].astype(jnp.int32) - 1, 0)
+        both = jnp.take_along_axis(state, jnp.broadcast_to(slot, (8, LANES)), axis=1, mode="promise_in_bounds")
+        state = in_box[p, 0:8, :] + both * in_box[p, 8:9, :]
+        for d in range(1, steps):
+            passed = jnp.where(place < 8 - 2 * d, in_box[p, 8 + d : 9 + d, :], 0.0)
+            state = state + pltpu.roll(both, 8 - 2 * d, 0) * passed
         back_box[p - 1] = state
 
-        @pl.when(me != p - 1)
+    home_box[me] = back_box[me]
+    for i in far[:-1]:
+        peer = peer_at(i)
+
+        @pl.when(peer < net - 1)
         def _():
-            homeward(p - 1, me).start()
-
-        @pl.when(me == p - 1)
-        def _():
-            home_box[p - 1] = back_box[p - 1]
+            homeward(peer, me).start()
+
+    @pl.when(me > 0)
+    def _():
+        across(me).wait_recv()
+
+    @pl.when(me == 0)
+    def _():
+        arrived[...] = jnp.zeros(arrived.shape, F32)
+
+    came = arrived[...].reshape(levels, members, LANES)
+    came = -0.5 * came[1:] - 0.3 * came[:steps]
+    boundary = jnp.sum(came * inside.reshape(steps, members, LANES), axis=0)
+    crossing = []
+    for t in range(steps):
+        weighted = came[t] * facts[0:1]
+        for d in range(1, t + 1):
+            weighted = weighted + came[t - d] * facts[d : d + 1]
+        crossing.append(weighted)
+    crossing = jnp.concatenate(crossing, 0)
 
     @pl.when(me == net - 1)
     def _():
@@ -277,97 +315,95 @@
 
             outer[pl.ds(k, 8, stride=stride), :] = home_box[k]
 
-    both = stack_split(outer[...])
-
-    def taken_at(slot):
-        return halves(dot(both, pick(slot))).reshape(steps, members, LANES)
+    both = jnp.concatenate(split(outer[...]), 1)
+
+    def taken_at(slots):
+        picked = jnp.concatenate([pick(slot) for slot in slots], 1)
+        return dot(both, jnp.concatenate([picked, picked], 0))
+
+    def weigh(g, carried):
+        out = []
+        for j in range(0, GROUP, 2):
+            lanes = pl.ds(pl.multiple_of(g * WIDE + j * LANES, 2 * LANES), 2 * LANES)
+            slots = gain[4:5, lanes]
+            value = taken_at([slots[:, :LANES], slots[:, LANES:]]).reshape(steps, members, 2 * LANES)
+            taken[:, :, lanes] = value
+            value = jnp.sum(jnp.sum(value * term[:, :, lanes], axis=0), axis=0, keepdims=True)
+            out += [value[:, :LANES], value[:, LANES:]]
+        here = pl.ds(pl.multiple_of(g * GROUP, GROUP), GROUP)
+        partial[here, :] += rows_of(out)
+        return carried
+
+    lax.fori_loop(0, groups, weigh, 0)
+
+    total = jnp.sum(taken_at([facts[4:5]]) * crossing, axis=0, keepdims=True) + jnp.sum(boundary, axis=0, keepdims=True)
+    size = partial.shape[0] // mem
+    for k in range(mem):
+        sum_out[k, 0:size, :] = partial[k * size : (k + 1) * size, :]
+        sum_out[k, size : size + 1, :] = total
+        sum_out[k, size + 1 :, :] = jnp.zeros((sum_out.shape[1] - size - 1, LANES), F32)
+    sum_in[you] = sum_out[you]
+    for i in range(1, mem):
+        sums(lax.rem(you + i, mem), you).start()
 
     def finish(g, carried):
-        side, scale = eight(table.at[4], g), eight(table.at[5], g)
-        out = []
+        side = eight(table.at[4], g)
         for j in range(GROUP):
             lanes = pl.ds(pl.multiple_of(g * WIDE + j * LANES, LANES), LANES)
             facts = gain[:, lanes]
-            taken = taken_at(facts[4:5])
-            total = jnp.zeros((members, LANES), F32)
+            value = taken[:, :, lanes]
             for t in range(steps):
                 adjoint = local[t, :, lanes]
                 for d in range(steps - t):
-                    adjoint = adjoint + facts[d : d + 1] * taken[t + d]
+                    adjoint = adjoint + facts[d : d + 1] * value[t + d]
                 grad[t, :, lanes] = (side[j : j + 1] * adjoint).astype(BF16)
-                total = total + adjoint * term[t, :, lanes]
-            out.append(jnp.sum(total, axis=0, keepdims=True))
-        partial[pl.ds(pl.multiple_of(g * GROUP, GROUP), GROUP), :] = rows_of(out)
         return carried
 
     lax.fori_loop(0, groups, finish, 0)
 
-    @pl.when(me > 0)
-    def _():
-        across(me).wait_recv()
-
-    @pl.when(me == 0)
-    def _():
-        arrived[...] = jnp.zeros(arrived.shape, F32)
-
-    came = arrived[...].reshape(levels, members, LANES)
-    came = -0.5 * came[1:] - 0.3 * came[:steps]
-    taken = taken_at(facts[4:5])
-    total = jnp.zeros((members, LANES), F32)
-    for t in range(steps):
-        adjoint = inside[t * members : (t + 1) * members]
-        for d in range(steps - t):
-            adjoint = adjoint + facts[d : d + 1] * taken[t + d]
-        total = total + adjoint * came[t]
-    total = jnp.sum(total, axis=0, keepdims=True)
-    high = total.astype(BF16).astype(F32)
-    total = rows_of([high, total - high]).astype(BF16)
-    within = lax.broadcasted_iota(jnp.int32, (LANES, LANES), 0)
-    lane = lax.broadcasted_iota(jnp.int32, (8, LANES), 1)
-    for g in range(groups):
-        out = []
-        for h in range(GROUP // 4):
-            first = (g * GROUP + h * 4) * LANES
-            near = jnp.where(within // 32 * LANES + within % 32 + first == inlet[...], 1.0, 0.0).astype(BF16)
-            placed = dot_t(total, near)
-            placed = placed + pltpu.roll(placed, 7, 0)
-            for i in range(4):
-                shifted = placed if i == 0 else pltpu.roll(placed, LANES - 32 * i, 1)
-                out.append(jnp.where(lane < 32, shifted, 0.0)[0:1])
-        here = pl.ds(g * GROUP, GROUP)
-        partial[here, :] = (partial[here, :] + rows_of(out)) * table[5, here, :]
-
-    for k in range(mem):
-        sum_out[k] = jnp.zeros((8, LANES), F32)
-        sum_out[k, 0:2, :] = partial[2 * k : 2 * k + 2, :]
-    sum_in[you] = sum_out[you]
-    for i in range(1, mem):
-        sums(lax.rem(you + i, mem), you).start()
     for i in range(1, mem):
         peer = lax.rem(you + i, mem)
         sums(peer, peer).wait_recv()
     total = sum_in[0]
     for k in range(1, mem):
         total = total + sum_in[k]
-    rough_out[...] = total[0:2]
+    edge_row = total[size : size + 1]
+    edge_high = edge_row.astype(BF16).astype(F32)
+    edge_row = rows_of([edge_high, edge_row - edge_high]).astype(BF16)
+    for i in range(size):
+        block = you * size + i
+        placed = dot_t(edge_row, one_hot(inlet[...], block * LANES))
+        rough_out[i : i + 1, :] = (total[i : i + 1] + placed[0:1] + placed[1:2]) * table[5, pl.ds(block, 1), :]
 
     for i in range(1, mem):
         sums(lax.rem(you + i, mem), you).wait_send()
 
     @pl.when(me > 0)
     def _():
-        for i in range(1, net):
-            outward(lax.rem(me + i, net), me).wait_send()
+        for i in far[:-1]:
+            outward(peer_at(i), me).wait_send()
 
     @pl.when(me < net - 1)
     def _():
         across(me + 1).wait_send()
 
-    for p in range(net - 1):
-
-        @pl.when(me != p)
+    for i in far[:-1]:
+        peer = peer_at(i)
+
+        @pl.when(peer < net - 1)
         def _():
-            homeward(p, me).wait_send()
+            homeward(peer, me).wait_send()
+
+
+def store_kernel(grad, rough, grad_out, rough_out, sem):
+    copies = [
+        pltpu.make_async_copy(grad, grad_out, sem.at[0]),
+        pltpu.make_async_copy(rough, rough_out, sem.at[1]),
+    ]
+    for copy in copies:
+        copy.start()
+    for copy in copies:
+        copy.wait()
 
 
 def body(stored_reach_flows, lateral, cotangent, roughness, travel_factor, inverse_block_matrix, down_in_block, exit_slot, inlet_reach):
@@ -390,8 +426,8 @@
         in_specs=[anywhere] * 9,
         out_specs=[vmem, vmem],
         out_shape=[
-            jax.ShapeDtypeStruct((steps, members, reaches), BF16),
-            jax.ShapeDtypeStruct((2, LANES), F32),
+            pltpu.VMEM((steps, members, reaches), BF16),
+            pltpu.VMEM((blocks // mem, LANES), F32),
         ],
         scratch_shapes=[
             shaped((steps, members, reaches), BF16),
@@ -405,7 +441,8 @@
             shaped((steps, members, reaches), F32),
             shaped((8, reaches), F32),
             shaped((steps, members, reaches), F32),
-            shaped((2 * (steps * members + 8), LANES), F32),
+            shaped((steps, members, reaches), F32),
+            shaped((steps * members + 8, LANES), F32),
             shaped((levels * members, LANES), F32),
             shaped((levels * members, LANES), F32),
             shaped((steps * members, LANES), F32),
@@ -415,8 +452,8 @@
             shaped((net, 8, LANES), F32),
             shaped((net, 8, LANES), F32),
             shaped((blocks, LANES), F32),
-            shaped((mem, 8, LANES), F32),
-            shaped((mem, 8, LANES), F32),
+            shaped((mem, 4, LANES), F32),
+            shaped((mem, 4, LANES), F32),
             dma((5,)), dma((groups,)), dma((groups,)), dma((groups,)), dma((groups,)),
             dma((net,)), dma((net,)), dma((net,)), dma((net,)), dma((2,)), dma((mem,)), dma((mem,)),
         ],
@@ -426,7 +463,19 @@
         cotangent, stored_reach_flows, lateral, inverse_block_matrix, blocked(roughness), blocked(travel_factor),
         blocked(exit_slot), blocked(down_in_block), inlet_reach,
     )
-    return grad_lateral, grad_rough.reshape(2 * LANES)
+    grad_lateral, grad_rough = pl.pallas_call(
+        store_kernel,
+        in_specs=[vmem, vmem],
+        out_specs=[anywhere, anywhere],
+        out_shape=[
+            jax.ShapeDtypeStruct(grad_lateral.shape, BF16),
+            jax.ShapeDtypeStruct(grad_rough.shape, F32),
+        ],
+        scratch_shapes=[dma((2,))],
+        compiler_params=pltpu.CompilerParams(vmem_limit_bytes=4 << 20),
+        name="store",
+    )(grad_lateral, grad_rough)
+    return grad_lateral, grad_rough.reshape(reaches // mem)
 
 
 def solution(mesh):

time: 39.1 us -> 33.1 us (0.85)
  Pallas kernels: 35.4 us -> 32.3 us
  local copies, waits for them, and re-layouts: 2.86 us -> 0 us
    pallas_call x1, Pallas kernels: 35.4 us -> 31.3 us  [body(): pl.pallas_call(kernel, in_specs=[anywhere] * 9, out_specs=[vmem, vmem], o...]
    unnamed x4 -> x0, local copies, waits for them, and re-layouts: 2.86 us -> none
    pallas_call x0 -> x1, Pallas kernels: none -> 0.99 us  [body(): pl.pallas_call(store_kernel, in_specs=[vmem, vmem], out_specs=[anywhere,...]
where the time goes in v3:
time: 33.1 us; the launch traced here: 32.9 us
  Pallas kernels  32.3 us (98%)
  between operations  0.64 us (2%)
    pallas_call x1, Pallas kernels, body(): pl.pallas_call(kernel, in_specs=[anywhere] * 9, out_specs=[vmem, vmem], o...  31.3 us
    pallas_call x1, Pallas kernels, body(): pl.pallas_call(store_kernel, in_specs=[vmem, vmem], out_specs=[anywhere,...  0.99 us

profile of v3, /device:TPU:1, one launch (start us, length us, event | category | flops | bytes accessed | tf_op | source)
XLA Modules:
  0.0 32.9 jit_solution(18018379127015405569)
XLA Ops:
  0.6 31.3 %adjoint.1 = (bf16[4,32,4096]{2,1,0:T(8,128)(2,1)S(1)}, f32[2,128]{1,0:T(2,128)S(1)}) custom-call(bf16[4,32,4096]{2,1,0:T(8,128)(2,1)} %cot_hbm.1, bf16[5,32,4096]{2,1,0:T(8,128)(2,1)} %flow_hbm.1, bf16[4,32,4096]{2,1,0:T(8,128)(2,1)} %lateral_hbm.1, f32[32,128,128]{2,1,0:T(8,128)} %matrix_hbm.1, f32[32,128]{1,0:T(8,128)} %bitcast.5, f32[32,128]{1,0:T(8,128)} %bitcast.6, ...), custom_call_target="tpu_custom_call" | custom-call | tf_op jit(solution)/shard_map/adjoint/pallas_call | solution.py:424
  31.9 1.0 %store.1 = (bf16[4,32,4096]{2,1,0:T(8,128)(2,1)}, f32[2,128]{1,0:T(2,128)}) custom-call(bf16[4,32,4096]{2,1,0:T(8,128)(2,1)S(1)} %get-tuple-element.6.grad, f32[2,128]{1,0:T(2,128)S(1)} %get-tuple-element.7.rough), custom_call_target="tpu_custom_call" | custom-call | tf_op jit(solution)/shard_map/store/pallas_call | solution.py:466

commit v4 on v3

--- a/solution.py
+++ b/solution.py
@@ -7,7 +7,7 @@
 
 F32, BF16 = jnp.float32, jnp.bfloat16
 LANES = 128
-GROUP = 8
+GROUP = 16
 WIDE = GROUP * LANES
 MESH = pl.DeviceIdType.MESH
 
@@ -36,6 +36,8 @@
 
 
 def rows_of(rows):
+    if len(rows) > 8:
+        return jnp.concatenate([rows_of(rows[:8]), rows_of(rows[8:])], 0)
     place = lax.broadcasted_iota(jnp.int32, (8, LANES), 0)
     out = jnp.zeros((8, LANES), F32)
     for i, row in enumerate(rows):
@@ -48,16 +50,15 @@
     return jnp.where(place == row, 1.0, 0.0).astype(BF16)
 
 
-def pick(slot):
-    number = lax.broadcasted_iota(jnp.int32, (LANES, LANES), 0).astype(F32) + 1.0
-    return jnp.where(number == slot, 1.0, 0.0).astype(BF16)
+def gather(value, row):
+    return jnp.take_along_axis(value, jnp.broadcast_to(row, value.shape), axis=1, mode="promise_in_bounds")
 
 
 def kernel(
     cot_hbm, flow_hbm, lateral_hbm, matrix_hbm, rough_hbm, factor_hbm, exits_hbm, down_hbm, inlet_hbm,
     grad, rough_out,
     cot, flow, lateral, matrix, rough, factor, exits, down, inlet,
-    table, local, gain, term, taken, inner, leaving, arrived, edge, outer,
+    table, local, gain, term, taken, inner, leaving, passing, arrived, edge, outer,
     out_box, in_box, back_box, home_box, partial, sum_out, sum_in,
     small_sem, matrix_sem, cot_sem, flow_sem, lateral_sem,
     send, recv, back_send, back_recv, cross_sem, sum_send, sum_recv,
@@ -70,6 +71,22 @@
     groups = reaches // WIDE
     me, you = lax.axis_index("net"), lax.axis_index("mem")
 
+    near = sorted(range(1, mem), key=lambda i: -(i // 8 + min(i % 8 // 2, 4 - i % 8 // 2)))
+
+    def mate_at(i):
+        y = lax.rem(lax.rem(you // 2, 4) + i % 8 // 2, 4)
+        return lax.rem(you // 8 + i // 8, 2) * 8 + y * 2 + lax.rem(lax.rem(you, 2) + i % 2, 2)
+
+    far = sorted(range(net), key=lambda i: -(2 * (i % 2) + min(i // 2, net // 2 - i // 2)))
+    high, low = me // 2, lax.rem(me, 2)
+
+    def peer_at(i):
+        return 2 * lax.rem(high + i // 2, net // 2) + lax.rem(low + i % 2, 2)
+
+    barrier = pltpu.get_barrier_semaphore()
+    for i in far[:-1]:
+        pl.semaphore_signal(barrier, inc=1, device_id={"net": peer_at(i)}, device_id_type=MESH)
+
     smalls = [
         pltpu.make_async_copy(a, b, small_sem.at[i])
         for i, (a, b) in enumerate(
@@ -92,16 +109,12 @@
     for g in range(groups):
         matrix_copy(g).start()
         wide_copy(cot_hbm, cot, cot_sem, g).start()
+    for i in near:
+        pl.semaphore_signal(barrier, inc=1, device_id={"mem": mate_at(i)}, device_id_type=MESH)
     smalls[4].start()
     for g in range(groups):
         wide_copy(flow_hbm, flow, flow_sem, g).start()
         wide_copy(lateral_hbm, lateral, lateral_sem, g).start()
-
-    barrier = pltpu.get_barrier_semaphore()
-    for i in range(1, net):
-        pl.semaphore_signal(barrier, inc=1, device_id={"net": lax.rem(me + i, net)}, device_id_type=MESH)
-    for i in range(1, mem):
-        pl.semaphore_signal(barrier, inc=1, device_id={"mem": lax.rem(you + i, mem)}, device_id_type=MESH)
 
     for copy in smalls[:4]:
         copy.wait()
@@ -158,15 +171,13 @@
                 found[j][t] = value[:members]
                 local[t, :, lanes[j]] = value[:members]
                 gains[j].append(value[members : members + 1])
-        pieces, marks = [], []
+        total = inner[...]
         for j in range(GROUP):
             facts = rows_of(gains[j] + [slots[j], weight_new[j : j + 1], weight_old[j : j + 1]])
             gain[:, lanes[j]] = facts
-            both = split(jnp.concatenate(found[j] + [facts], 0))
-            mark = one_hot(inlet[...], (g * GROUP + j) * LANES)
-            pieces += both
-            marks += [mark, mark]
-        inner[...] += dot(jnp.concatenate(pieces, 1), jnp.concatenate(marks, 0))
+            value = gather(jnp.concatenate(found[j] + [facts], 0), lax.rem(inlet[...], LANES))
+            total = jnp.where(inlet[...] // LANES == g * GROUP + j, value, total)
+        inner[...] = total
         return carried
 
     lax.fori_loop(0, groups, solve, 0)
@@ -185,15 +196,9 @@
         out_box[k, 8:16, :] = message
     in_box[me] = out_box[me]
 
-    far = sorted(range(net), key=lambda i: -(2 * (i % 2) + min(i // 2, net // 2 - i // 2)))
-    high, low = me // 2, lax.rem(me, 2)
-
-    def peer_at(i):
-        return 2 * lax.rem(high + i // 2, net // 2) + lax.rem(low + i % 2, 2)
-
     def outward(peer, slot):
         return pltpu.make_async_remote_copy(
-            src_ref=out_box.at[peer], dst_ref=in_box.at[slot], send_sem=send.at[peer], recv_sem=recv.at[slot],
+            src_ref=out_box.at[peer, 0 : 8 + levels], dst_ref=in_box.at[slot, 0 : 8 + levels], send_sem=send.at[peer], recv_sem=recv.at[slot],
             device_id={"net": peer}, device_id_type=MESH,
         )
 
@@ -205,7 +210,7 @@
 
     def across(peer):
         return pltpu.make_async_remote_copy(
-            src_ref=leaving, dst_ref=arrived, send_sem=cross_sem.at[0], recv_sem=cross_sem.at[1],
+            src_ref=passing, dst_ref=arrived, send_sem=cross_sem.at[0], recv_sem=cross_sem.at[1],
             device_id={"net": peer}, device_id_type=MESH,
         )
 
@@ -252,9 +257,8 @@
 
     lax.fori_loop(0, groups, inflows, 0)
 
-    @pl.when(me < net - 1)
-    def _():
-        across(me + 1).start()
+    crossed = leaving[...]
+    passing[...] = -0.5 * crossed[members:] - 0.3 * crossed[:rows]
 
     for p in range(1, net):
 
@@ -267,7 +271,7 @@
     back_box[net - 2] = state
     for p in reversed(range(1, net - 1)):
         slot = jnp.maximum(in_box[p, 12:13, :].astype(jnp.int32) - 1, 0)
-        both = jnp.take_along_axis(state, jnp.broadcast_to(slot, (8, LANES)), axis=1, mode="promise_in_bounds")
+        both = gather(state, slot)
         state = in_box[p, 0:8, :] + both * in_box[p, 8:9, :]
         for d in range(1, steps):
             passed = jnp.where(place < 8 - 2 * d, in_box[p, 8 + d : 9 + d, :], 0.0)
@@ -282,6 +286,40 @@
         def _():
             homeward(peer, me).start()
 
+    @pl.when(me < net - 1)
+    def _():
+        across(me + 1).start()
+
+    @pl.when(me == net - 1)
+    def _():
+        outer[...] = jnp.zeros(outer.shape, F32)
+
+    @pl.when(me < net - 1)
+    def _():
+        for k in range(net):
+
+            @pl.when(me != k)
+            def _():
+                homeward(k, k).wait_recv()
+
+            outer[pl.ds(k, 8, stride=stride), :] = home_box[k]
+
+    def taken_at(slot):
+        return gather(outer[...], jnp.maximum(slot.astype(jnp.int32) - 1, 0))
+
+    def weigh(g, carried):
+        out = []
+        for j in range(GROUP):
+            lanes = pl.ds(pl.multiple_of(g * WIDE + j * LANES, LANES), LANES)
+            value = taken_at(gain[4:5, lanes]).reshape(steps, members, LANES)
+            taken[:, :, lanes] = value
+            out.append(jnp.sum(jnp.sum(value * term[:, :, lanes], axis=0), axis=0, keepdims=True))
+        here = pl.ds(pl.multiple_of(g * GROUP, GROUP), GROUP)
+        partial[here, :] += rows_of(out)
+        return carried
+
+    lax.fori_loop(0, groups, weigh, 0)
+
     @pl.when(me > 0)
     def _():
         across(me).wait_recv()
@@ -290,8 +328,7 @@
     def _():
         arrived[...] = jnp.zeros(arrived.shape, F32)
 
-    came = arrived[...].reshape(levels, members, LANES)
-    came = -0.5 * came[1:] - 0.3 * came[:steps]
+    came = arrived[...].reshape(steps, members, LANES)
     boundary = jnp.sum(came * inside.reshape(steps, members, LANES), axis=0)
     crossing = []
     for t in range(steps):
@@ -301,50 +338,15 @@
         crossing.append(weighted)
     crossing = jnp.concatenate(crossing, 0)
 
-    @pl.when(me == net - 1)
-    def _():
-        outer[...] = jnp.zeros(outer.shape, F32)
-
-    @pl.when(me < net - 1)
-    def _():
-        for k in range(net):
-
-            @pl.when(me != k)
-            def _():
-                homeward(k, k).wait_recv()
-
-            outer[pl.ds(k, 8, stride=stride), :] = home_box[k]
-
-    both = jnp.concatenate(split(outer[...]), 1)
-
-    def taken_at(slots):
-        picked = jnp.concatenate([pick(slot) for slot in slots], 1)
-        return dot(both, jnp.concatenate([picked, picked], 0))
-
-    def weigh(g, carried):
-        out = []
-        for j in range(0, GROUP, 2):
-            lanes = pl.ds(pl.multiple_of(g * WIDE + j * LANES, 2 * LANES), 2 * LANES)
-            slots = gain[4:5, lanes]
-            value = taken_at([slots[:, :LANES], slots[:, LANES:]]).reshape(steps, members, 2 * LANES)
-            taken[:, :, lanes] = value
-            value = jnp.sum(jnp.sum(value * term[:, :, lanes], axis=0), axis=0, keepdims=True)
-            out += [value[:, :LANES], value[:, LANES:]]
-        here = pl.ds(pl.multiple_of(g * GROUP, GROUP), GROUP)
-        partial[here, :] += rows_of(out)
-        return carried
-
-    lax.fori_loop(0, groups, weigh, 0)
-
-    total = jnp.sum(taken_at([facts[4:5]]) * crossing, axis=0, keepdims=True) + jnp.sum(boundary, axis=0, keepdims=True)
+    total = jnp.sum(taken_at(facts[4:5]) * crossing, axis=0, keepdims=True) + jnp.sum(boundary, axis=0, keepdims=True)
     size = partial.shape[0] // mem
     for k in range(mem):
         sum_out[k, 0:size, :] = partial[k * size : (k + 1) * size, :]
         sum_out[k, size : size + 1, :] = total
         sum_out[k, size + 1 :, :] = jnp.zeros((sum_out.shape[1] - size - 1, LANES), F32)
     sum_in[you] = sum_out[you]
-    for i in range(1, mem):
-        sums(lax.rem(you + i, mem), you).start()
+    for i in near:
+        sums(mate_at(i), you).start()
 
     def finish(g, carried):
         side = eight(table.at[4], g)
@@ -444,7 +446,8 @@
             shaped((steps, members, reaches), F32),
             shaped((steps * members + 8, LANES), F32),
             shaped((levels * members, LANES), F32),
-            shaped((levels * members, LANES), F32),
+            shaped((steps * members, LANES), F32),
+            shaped((steps * members, LANES), F32),
             shaped((steps * members, LANES), F32),
             shaped((steps * members, LANES), F32),
             shaped((net, 16, LANES), F32),

time: 33.1 us -> 32.1 us (0.970)
  Pallas kernels: 32.3 us -> 31.3 us
    pallas_call x1, Pallas kernels: 31.3 us -> 30.3 us  [body(): pl.pallas_call(kernel, in_specs=[anywhere] * 9, out_specs=[vmem, vmem], o...]
where the time goes in v4:
time: 32.1 us; the launch traced here: 32 us
  Pallas kernels  31.3 us (98%)
  between operations  0.64 us (2%)
    pallas_call x1, Pallas kernels, body(): pl.pallas_call(kernel, in_specs=[anywhere] * 9, out_specs=[vmem, vmem], o...  30.3 us
    pallas_call x1, Pallas kernels, body(): pl.pallas_call(store_kernel, in_specs=[vmem, vmem], out_specs=[anywhere,...  0.99 us

profile of v4, /device:TPU:1, one launch (start us, length us, event | category | flops | bytes accessed | tf_op | source)
XLA Modules:
  0.0 32.0 jit_solution(6787030143982622261)
XLA Ops:
  0.6 30.3 %adjoint.1 = (bf16[4,32,4096]{2,1,0:T(8,128)(2,1)S(1)}, f32[2,128]{1,0:T(2,128)S(1)}) custom-call(bf16[4,32,4096]{2,1,0:T(8,128)(2,1)} %cot_hbm.1, bf16[5,32,4096]{2,1,0:T(8,128)(2,1)} %flow_hbm.1, bf16[4,32,4096]{2,1,0:T(8,128)(2,1)} %lateral_hbm.1, f32[32,128,128]{2,1,0:T(8,128)} %matrix_hbm.1, f32[32,128]{1,0:T(8,128)} %bitcast.5, f32[32,128]{1,0:T(8,128)} %bitcast.6, ...), custom_call_target="tpu_custom_call" | custom-call | tf_op jit(solution)/shard_map/adjoint/pallas_call | solution.py:426
  31.0 1.0 %store.1 = (bf16[4,32,4096]{2,1,0:T(8,128)(2,1)}, f32[2,128]{1,0:T(2,128)}) custom-call(bf16[4,32,4096]{2,1,0:T(8,128)(2,1)S(1)} %get-tuple-element.6.grad, f32[2,128]{1,0:T(2,128)S(1)} %get-tuple-element.7.rough), custom_call_target="tpu_custom_call" | custom-call | tf_op jit(solution)/shard_map/store/pallas_call | solution.py:469

commit v5 on v4

--- a/solution.py
+++ b/solution.py
@@ -63,11 +63,12 @@
     small_sem, matrix_sem, cot_sem, flow_sem, lateral_sem,
     send, recv, back_send, back_recv, cross_sem, sum_send, sum_recv,
 ):
-    net, mem = out_box.shape[0], sum_out.shape[0]
+    net, mem = in_box.shape[0], sum_out.shape[0]
+    spots = out_box.shape[0]
+    lines = home_box.shape[1]
     steps, members, reaches = cot.shape
     levels = steps + 1
     rows = steps * members
-    stride = rows // 8
     groups = reaches // WIDE
     me, you = lax.axis_index("net"), lax.axis_index("mem")
 
@@ -77,11 +78,12 @@
         y = lax.rem(lax.rem(you // 2, 4) + i % 8 // 2, 4)
         return lax.rem(you // 8 + i // 8, 2) * 8 + y * 2 + lax.rem(lax.rem(you, 2) + i % 2, 2)
 
-    far = sorted(range(net), key=lambda i: -(2 * (i % 2) + min(i // 2, net // 2 - i // 2)))
+    far = sorted(range(net), key=lambda i: -(2 * (i % 2) + min(i // 2, spots - i // 2)))
+    far_home = [i for i in far if i % 2 == 0]
     high, low = me // 2, lax.rem(me, 2)
 
     def peer_at(i):
-        return 2 * lax.rem(high + i // 2, net // 2) + lax.rem(low + i % 2, 2)
+        return 2 * lax.rem(high + i // 2, spots) + lax.rem(low + i % 2, 2)
 
     barrier = pltpu.get_barrier_semaphore()
     for i in far[:-1]:
@@ -191,21 +193,21 @@
     )
     passed = [weight_new * facts[0:1]] + [weight_new * facts[d : d + 1] + weight_old * facts[d - 1 : d] for d in range(1, steps)]
     message = rows_of(passed + [facts[4:5]])
-    for k in range(net):
-        out_box[k, 0:8, :] = edge[pl.ds(k, 8, stride=stride), :]
-        out_box[k, 8:16, :] = message
-    in_box[me] = out_box[me]
+    for k in range(spots):
+        out_box[k, 0:lines, :] = edge[pl.ds(k, lines, stride=spots), :]
+        out_box[k, lines : lines + 8, :] = message
+    in_box[me] = out_box[high]
 
     def outward(peer, slot):
         return pltpu.make_async_remote_copy(
-            src_ref=out_box.at[peer, 0 : 8 + levels], dst_ref=in_box.at[slot, 0 : 8 + levels], send_sem=send.at[peer], recv_sem=recv.at[slot],
+            src_ref=out_box.at[peer // 2, 0 : lines + levels], dst_ref=in_box.at[slot, 0 : lines + levels], send_sem=send.at[peer], recv_sem=recv.at[slot],
             device_id={"net": peer}, device_id_type=MESH,
         )
 
     def homeward(peer, slot):
         return pltpu.make_async_remote_copy(
-            src_ref=back_box.at[peer], dst_ref=home_box.at[slot], send_sem=back_send.at[peer],
-            recv_sem=back_recv.at[slot], device_id={"net": peer}, device_id_type=MESH,
+            src_ref=back_box.at[peer], dst_ref=home_box.at[slot // 2], send_sem=back_send.at[peer],
+            recv_sem=back_recv.at[slot // 2], device_id={"net": peer}, device_id_type=MESH,
         )
 
     def across(peer):
@@ -266,20 +268,21 @@
         def _():
             outward(p, p).wait_recv()
 
-    place = lax.broadcasted_iota(jnp.int32, (8, LANES), 0)
-    state = in_box[net - 1, 0:8, :]
+    later = lines // steps
+    place = lax.broadcasted_iota(jnp.int32, (lines, LANES), 0)
+    state = in_box[net - 1, 0:lines, :]
     back_box[net - 2] = state
     for p in reversed(range(1, net - 1)):
-        slot = jnp.maximum(in_box[p, 12:13, :].astype(jnp.int32) - 1, 0)
+        slot = jnp.maximum(in_box[p, lines + steps : lines + levels, :].astype(jnp.int32) - 1, 0)
         both = gather(state, slot)
-        state = in_box[p, 0:8, :] + both * in_box[p, 8:9, :]
+        state = in_box[p, 0:lines, :] + both * in_box[p, lines : lines + 1, :]
         for d in range(1, steps):
-            passed = jnp.where(place < 8 - 2 * d, in_box[p, 8 + d : 9 + d, :], 0.0)
-            state = state + pltpu.roll(both, 8 - 2 * d, 0) * passed
+            passed = jnp.where(place < lines - later * d, in_box[p, lines + d : lines + d + 1, :], 0.0)
+            state = state + pltpu.roll(both, lines - later * d, 0) * passed
         back_box[p - 1] = state
 
-    home_box[me] = back_box[me]
-    for i in far[:-1]:
+    home_box[high] = back_box[me]
+    for i in far_home[:-1]:
         peer = peer_at(i)
 
         @pl.when(peer < net - 1)
@@ -290,19 +293,37 @@
     def _():
         across(me + 1).start()
 
+    @pl.when(me > 0)
+    def _():
+        across(me).wait_recv()
+
+    @pl.when(me == 0)
+    def _():
+        arrived[...] = jnp.zeros(arrived.shape, F32)
+
+    came = arrived[...].reshape(steps, members, LANES)
+    boundary = jnp.sum(came * inside.reshape(steps, members, LANES), axis=0)
+    crossing = []
+    for t in range(steps):
+        weighted = came[t] * facts[0:1]
+        for d in range(1, t + 1):
+            weighted = weighted + came[t - d] * facts[d : d + 1]
+        crossing.append(weighted)
+    crossing = jnp.concatenate(crossing, 0)
+
     @pl.when(me == net - 1)
     def _():
         outer[...] = jnp.zeros(outer.shape, F32)
 
     @pl.when(me < net - 1)
     def _():
-        for k in range(net):
-
-            @pl.when(me != k)
+        for k in range(spots):
+
+            @pl.when(high != k)
             def _():
-                homeward(k, k).wait_recv()
-
-            outer[pl.ds(k, 8, stride=stride), :] = home_box[k]
+                homeward(2 * k, 2 * k).wait_recv()
+
+            outer[pl.ds(k, lines, stride=spots), :] = home_box[k]
 
     def taken_at(slot):
         return gather(outer[...], jnp.maximum(slot.astype(jnp.int32) - 1, 0))
@@ -319,24 +340,6 @@
         return carried
 
     lax.fori_loop(0, groups, weigh, 0)
-
-    @pl.when(me > 0)
-    def _():
-        across(me).wait_recv()
-
-    @pl.when(me == 0)
-    def _():
-        arrived[...] = jnp.zeros(arrived.shape, F32)
-
-    came = arrived[...].reshape(steps, members, LANES)
-    boundary = jnp.sum(came * inside.reshape(steps, members, LANES), axis=0)
-    crossing = []
-    for t in range(steps):
-        weighted = came[t] * facts[0:1]
-        for d in range(1, t + 1):
-            weighted = weighted + came[t - d] * facts[d : d + 1]
-        crossing.append(weighted)
-    crossing = jnp.concatenate(crossing, 0)
 
     total = jnp.sum(taken_at(facts[4:5]) * crossing, axis=0, keepdims=True) + jnp.sum(boundary, axis=0, keepdims=True)
     size = partial.shape[0] // mem
@@ -389,7 +392,7 @@
     def _():
         across(me + 1).wait_send()
 
-    for i in far[:-1]:
+    for i in far_home[:-1]:
         peer = peer_at(i)
 
         @pl.when(peer < net - 1)
@@ -398,10 +401,11 @@
 
 
 def store_kernel(grad, rough, grad_out, rough_out, sem):
-    copies = [
-        pltpu.make_async_copy(grad, grad_out, sem.at[0]),
-        pltpu.make_async_copy(rough, rough_out, sem.at[1]),
-    ]
+    copies = [pltpu.make_async_copy(rough, rough_out, sem.at[0])]
+    pieces = sem.shape[0] - 1
+    for i in range(pieces):
+        part = (i // 2, slice(None), slice(i % 2 * (grad.shape[2] // 2), (i % 2 + 1) * (grad.shape[2] // 2)))
+        copies.append(pltpu.make_async_copy(grad.at[part], grad_out.at[part], sem.at[i + 1]))
     for copy in copies:
         copy.start()
     for copy in copies:
@@ -414,6 +418,8 @@
     blocks = reaches // LANES
     groups = reaches // WIDE
     net, mem = lax.axis_size("net"), lax.axis_size("mem")
+    spots = net // 2
+    lines = steps * members // spots
 
     def blocked(value):
         return value.reshape(blocks, LANES)
@@ -450,10 +456,10 @@
             shaped((steps * members, LANES), F32),
             shaped((steps * members, LANES), F32),
             shaped((steps * members, LANES), F32),
-            shaped((net, 16, LANES), F32),
-            shaped((net, 16, LANES), F32),
-            shaped((net, 8, LANES), F32),
-            shaped((net, 8, LANES), F32),
+            shaped((spots, lines + 8, LANES), F32),
+            shaped((net, lines + 8, LANES), F32),
+            shaped((net, lines, LANES), F32),
+            shaped((spots, lines, LANES), F32),
             shaped((blocks, LANES), F32),
             shaped((mem, 4, LANES), F32),
             shaped((mem, 4, LANES), F32),
@@ -474,7 +480,7 @@
             jax.ShapeDtypeStruct(grad_lateral.shape, BF16),
             jax.ShapeDtypeStruct(grad_rough.shape, F32),
         ],
-        scratch_shapes=[dma((2,))],
+        scratch_shapes=[dma((2 * steps + 1,))],
         compiler_params=pltpu.CompilerParams(vmem_limit_bytes=4 << 20),
         name="store",
     )(grad_lateral, grad_rough)

time: 32.1 us -> 31.7 us (0.988)
  Pallas kernels: 31.3 us -> 30.9 us
    pallas_call x1, Pallas kernels: 30.3 us -> 29.8 us  [body(): pl.pallas_call(kernel, in_specs=[anywhere] * 9, out_specs=[vmem, vmem], o...]
where the time goes in v5:
time: 31.7 us; the launch traced here: 31.5 us
  Pallas kernels  30.9 us (97%)
  between operations  0.64 us (2%)
    pallas_call x1, Pallas kernels, body(): pl.pallas_call(kernel, in_specs=[anywhere] * 9, out_specs=[vmem, vmem], o...  29.8 us
    pallas_call x1, Pallas kernels, body(): pl.pallas_call(store_kernel, in_specs=[vmem, vmem], out_specs=[anywhere,...  1.04 us

profile of v5, /device:TPU:1, one launch (start us, length us, event | category | flops | bytes accessed | tf_op | source)
XLA Modules:
  0.0 31.5 jit_solution(2652461213248442154)
XLA Ops:
  0.6 29.8 %adjoint.1 = (bf16[4,32,4096]{2,1,0:T(8,128)(2,1)S(1)}, f32[2,128]{1,0:T(2,128)S(1)}) custom-call(bf16[4,32,4096]{2,1,0:T(8,128)(2,1)} %cot_hbm.1, bf16[5,32,4096]{2,1,0:T(8,128)(2,1)} %flow_hbm.1, bf16[4,32,4096]{2,1,0:T(8,128)(2,1)} %lateral_hbm.1, f32[32,128,128]{2,1,0:T(8,128)} %matrix_hbm.1, f32[32,128]{1,0:T(8,128)} %bitcast.5, f32[32,128]{1,0:T(8,128)} %bitcast.6, ...), custom_call_target="tpu_custom_call" | custom-call | tf_op jit(solution)/shard_map/adjoint/pallas_call | solution.py:432
  30.5 1.0 %store.1 = (bf16[4,32,4096]{2,1,0:T(8,128)(2,1)}, f32[2,128]{1,0:T(2,128)}) custom-call(bf16[4,32,4096]{2,1,0:T(8,128)(2,1)S(1)} %get-tuple-element.6.grad, f32[2,128]{1,0:T(2,128)S(1)} %get-tuple-element.7.rough), custom_call_target="tpu_custom_call" | custom-call | tf_op jit(solution)/shard_map/store/pallas_call | solution.py:475

commit v6 on v5

--- a/solution.py
+++ b/solution.py
@@ -7,7 +7,7 @@
 
 F32, BF16 = jnp.float32, jnp.bfloat16
 LANES = 128
-GROUP = 16
+GROUP = 32
 WIDE = GROUP * LANES
 MESH = pl.DeviceIdType.MESH
 
@@ -37,7 +37,7 @@
 
 def rows_of(rows):
     if len(rows) > 8:
-        return jnp.concatenate([rows_of(rows[:8]), rows_of(rows[8:])], 0)
+        return jnp.concatenate([rows_of(rows[i : i + 8]) for i in range(0, len(rows), 8)], 0)
     place = lax.broadcasted_iota(jnp.int32, (8, LANES), 0)
     out = jnp.zeros((8, LANES), F32)
     for i, row in enumerate(rows):

time: 31.7 us -> 31.7 us (level)
  no operation moved by 1% of the time
where the time goes in v6:
time: 31.7 us; the launch traced here: 31.6 us
  Pallas kernels  30.9 us (97%)
  between operations  0.64 us (2%)
    pallas_call x1, Pallas kernels, body(): pl.pallas_call(kernel, in_specs=[anywhere] * 9, out_specs=[vmem, vmem], o...  29.9 us
    pallas_call x1, Pallas kernels, body(): pl.pallas_call(store_kernel, in_specs=[vmem, vmem], out_specs=[anywhere,...  1.04 us

profile of v6, /device:TPU:1, one launch (start us, length us, event | category | flops | bytes accessed | tf_op | source)
XLA Modules:
  0.0 31.6 jit_solution(16407362175168606907)
XLA Ops:
  0.6 29.9 %adjoint.1 = (bf16[4,32,4096]{2,1,0:T(8,128)(2,1)S(1)}, f32[2,128]{1,0:T(2,128)S(1)}) custom-call(bf16[4,32,4096]{2,1,0:T(8,128)(2,1)} %cot_hbm.1, bf16[5,32,4096]{2,1,0:T(8,128)(2,1)} %flow_hbm.1, bf16[4,32,4096]{2,1,0:T(8,128)(2,1)} %lateral_hbm.1, f32[32,128,128]{2,1,0:T(8,128)} %matrix_hbm.1, f32[32,128]{1,0:T(8,128)} %bitcast.5, f32[32,128]{1,0:T(8,128)} %bitcast.6, ...), custom_call_target="tpu_custom_call" | custom-call | tf_op jit(solution)/shard_map/adjoint/pallas_call | solution.py:432
  30.5 1.0 %store.1 = (bf16[4,32,4096]{2,1,0:T(8,128)(2,1)}, f32[2,128]{1,0:T(2,128)}) custom-call(bf16[4,32,4096]{2,1,0:T(8,128)(2,1)S(1)} %get-tuple-element.6.grad, f32[2,128]{1,0:T(2,128)S(1)} %get-tuple-element.7.rough), custom_call_target="tpu_custom_call" | custom-call | tf_op jit(solution)/shard_map/store/pallas_call | solution.py:475
